TPU v7x, 256 devices: a whole 4x4x8 slice. The times are simulated.
256 devices in a mesh: ang: 8 (over x, z_hi), rad: 32 (over z_lo, y, core).
Axes of the slice: x: 4, y: 4, z: 8 (z_hi: 2, z_lo: 4; z = z_hi * 4 + z_lo), core: 2. Of those that a mesh axis runs over, the one named last changes fastest.
Arguments:
- psi_bound: bfloat16 [64, 64, 1024], P('rad', None, 'ang'), may hold values from -6 to 6
- psi_cont: bfloat16 [64, 512, 1024], P('rad', None, 'ang'), may hold values from -6 to 6
- ylm: bfloat16 [1024, 1024], P('ang'), may hold values from -0.1875 to 0.1875
- radial_weight: float32 [64], P('rad'), may hold values from 0.0003 to 0.003
- order: int32 [1024], replicated, may hold values from 0 to 1023, each once
Outputs:
- dipole: float32 [64, 512], P('ang', 'rad')
Inputs may be any that keep to these rules, and one draw needn't show every extreme that they name: order holds each of the 1024 harmonic indices exactly once.
All inputs are finite; a program needn't handle non-finite values.
Results may differ from a plain program's by a relative error of at most 0.029.
Values may be sent and summed in bfloat16 or wider, within the bound.
A program may use at most 64 MiB of HBM per device.

v0:
```python
import jax
import jax.numpy as jnp
from jax import lax
from jax.sharding import PartitionSpec as P

LMAX = 31


def over_pieces(array, axis):
    return lax.all_gather(array, axis).astype(jnp.float32).sum(0)


def cut_along(array, dim, devices):
    before, after = (array.shape[:dim], array.shape[dim + 1 :])
    return jnp.moveaxis(array.reshape(*before, devices, -1, *after), dim, 0)


def sent_and_summed(array, axis, dim):
    devices = lax.axis_size(axis)
    tiles = lax.all_to_all(cut_along(array, dim, devices), axis, 0, 0, tiled=True)
    return jnp.sum(tiles.astype(jnp.float32), axis=0)


def sent_and_summed_2(array, axis, dim):
    tiles = cut_along(array, dim, lax.axis_size(axis))
    arrived = lax.all_to_all(tiles, axis, split_axis=0, concat_axis=0, tiled=True)
    return arrived.sum(axis=0)


def harmonic_tables(order, total):
    columns = jnp.arange(total, dtype=jnp.int32)
    squares_list = jnp.arange(1, LMAX + 1, dtype=jnp.int32) ** 2
    degree = jnp.sum((order[:, None] >= squares_list[None, :]).astype(jnp.int32), axis=1)
    order_m = order - degree * degree - degree
    inverse = jnp.zeros((total,), jnp.int32).at[order].set(columns)
    degf = degree.astype(jnp.float32)
    mvalue = order_m.astype(jnp.float32)
    upper_l = degree + 1
    upper_ok = upper_l <= LMAX
    upper_idx = jnp.clip(upper_l * upper_l + upper_l + order_m, 0, total - 1)
    upper_col = inverse[upper_idx]
    upper_num = (degf + 1.0) ** 2 - mvalue**2
    upper_den = (2.0 * degf + 1.0) * (2.0 * degf + 3.0)
    upper_coef = jnp.where(upper_ok, jnp.sqrt(jnp.maximum(upper_num, 0.0) / upper_den), 0.0)
    lower_l = degree - 1
    lower_ok = lower_l >= jnp.abs(order_m)
    lower_idx = jnp.clip(lower_l * lower_l + lower_l + order_m, 0, total - 1)
    lower_col = inverse[lower_idx]
    lower_num = degf**2 - mvalue**2
    lower_den = jnp.maximum((2.0 * degf - 1.0) * (2.0 * degf + 1.0), 1.0)
    lower_coef = jnp.where(lower_ok, jnp.sqrt(jnp.maximum(lower_num, 0.0) / lower_den), 0.0)
    return (upper_col, upper_coef, lower_col, lower_coef)


def couple(values, tables):
    upper_col, upper_coef, lower_col, lower_coef = tables
    return values[..., upper_col] * upper_coef + values[..., lower_col] * lower_coef


def shards(psi_bound, psi_cont, ylm, radial_weight, order):
    shells, bound_count, points = psi_bound.shape
    cont_count = psi_cont.shape[1]
    total = ylm.shape[1]
    tables = harmonic_tables(order, total)
    cont_part = jnp.dot(
        psi_cont.reshape(shells * cont_count, points), ylm, preferred_element_type=jnp.float32
    )
    cont_part = cont_part.astype(jnp.bfloat16).reshape(shells, cont_count, total)
    bound_part = jnp.dot(
        psi_bound.reshape(shells * bound_count, points), ylm, preferred_element_type=jnp.float32
    )
    bound_part = (
        bound_part.astype(jnp.bfloat16).astype(jnp.float32).reshape(shells, bound_count, total)
    )
    bound_full = over_pieces(bound_part.astype(jnp.bfloat16), "ang").astype(jnp.float32)
    coupled = couple(bound_full, tables).astype(jnp.bfloat16)
    per_shell = jnp.einsum("rbk,rck->rbc", coupled, cont_part, preferred_element_type=jnp.float32)
    dipole_part = jnp.einsum("r,rbc->bc", radial_weight, per_shell, precision=lax.Precision.HIGHEST)
    across = sent_and_summed(dipole_part.astype(jnp.bfloat16), "rad", 1)
    result = sent_and_summed_2(across, "ang", 0)
    return result


def solution(mesh):
    return jax.shard_map(
        shards,
        mesh=mesh,
        in_specs=(P("rad", None, "ang"), P("rad", None, "ang"), P("ang", None), P("rad"), P()),
        out_specs=P("ang", "rad"),
        check_vma=False,
    )
```

profile of v0, /device:TPU:1, one launch (start us, length us, event | category | flops | bytes accessed | tf_op | source)
XLA Modules:
  0.0 151.4 jit_solution(7516237491783851033)
XLA Ops:
  6.5 2.0 %convolution_convert_fusion.1 = bf16[128,1024]{1,0:T(8,128)(2,1)} fusion(bf16[128,128]{1,0:T(8,128)(2,1)} %bitcast.34, bf16[128,1024]{1,0:T(8,128)(2,1)} %param.7), kind=kOutput, calls=%fused_computation.7 | convolution fusion | flops 33685504 | bytes 557056 | tf_op jit(solution)/shard_map/dot_general | solution.py:69
  8.5 0.0 all-gather.2.cloned.1.call-update
  8.5 0.7 compare_select_fusion.4
  9.2 4.3 %scatter_custom_fusion = s32[1024]{0:T(1024)S(1)} fusion(s32[1024]{0:T(1024)S(1)} %compare_select_fusion.4, s32[1024]{0:T(1024)S(1)} %iota.8, s32[]{:T(128)} %constant.2.clone.1), kind=kCustom, calls=%fused_computation.40 | custom fusion | bytes 4100 | tf_op jit(solution)/shard_map/scatter | solution.py:35
  13.5 0.8 convert_reduce_fusion.2
  14.3 0.7 sqrt_select_fusion.1
  15.0 4.5 %gather_fusion = s32[1024]{0:T(1024)S(1)} fusion(s32[1024]{0:T(1024)S(1)} %scatter_custom_fusion, s32[1024]{0:T(1024)S(1)} %get-tuple-element.7), kind=kCustom, calls=%fused_computation | custom fusion | bytes 12288 | tf_op jit(solution)/shard_map/gather | solution.py:41
  19.6 0.0 copy-start.1
  19.6 4.5 %gather_fusion.2 = s32[1024]{0:T(1024)S(1)} fusion(s32[1024]{0:T(1024)S(1)} %scatter_custom_fusion, s32[1024]{0:T(1024)S(1)} %get-tuple-element.8), kind=kCustom, calls=%fused_computation.2 | custom fusion | bytes 12288 | tf_op jit(solution)/shard_map/gather | solution.py:48
  24.2 0.7 convolution_convert_fusion
  24.9 63.8 %all-gather.2.cloned.1.call-done = bf16[8,2,64,1024]{3,2,1,0:T(8,128)(2,1)} async-done(((bf16[1,2,64,1024]{3,2,1,0:T(8,128)(2,1)}), bf16[8,2,64,1024]{3,2,1,0:T(8,128)(2,1)}) %all-gather.2.cloned.1.call-update) | async-done | bytes 2097168 | tf_op jit(solution)/shard_map/all_gather | solution.py:10
  88.7 2.8 %convert_reduce_fusion = f32[2,64,1024]{2,1,0:T(8,128)} fusion(bf16[8,2,64,1024]{3,2,1,0:T(8,128)(2,1)} %all-gather.2.cloned.1.call-done), kind=kLoop, calls=%fused_computation.5 | loop fusion | flops 1966080 | bytes 2621440 | tf_op jit(solution)/shard_map/reduce_sum | solution.py:10
  91.5 1.4 copy.17
  92.9 7.5 %gather_fusion.1 = f32[1024,2,64]{2,1,0:T(2,128)} fusion(f32[2,64,1024]{1,0,2:T(2,128)S(1)} %copy.17, s32[1024]{0:T(1024)S(1)} %broadcast_clamp_fusion.1), kind=kCustom, calls=%fused_computation.1 | custom fusion | bytes 1052672 | tf_op jit(solution)/shard_map/gather | solution.py:57
  100.4 2.1 %copy.18 = f32[1024,2,64]{0,2,1:T(8,128)} copy(f32[1024,2,64]{2,1,0:T(2,128)} %gather_fusion.1) | data formatting | bytes 1048576 | tf_op jit(solution)/shard_map/gather | solution.py:57
  102.6 7.5 %gather_fusion.3 = f32[1024,2,64]{2,1,0:T(2,128)} fusion(f32[2,64,1024]{1,0,2:T(2,128)S(1)} %copy.17, s32[1024]{0:T(1024)S(1)} %broadcast_clamp_fusion), kind=kCustom, calls=%fused_computation.3 | custom fusion | bytes 1052672 | tf_op jit(solution)/shard_map/gather | solution.py:57
  110.1 1.4 copy.20
  111.5 0.0 copy-start.2
  111.5 1.8 %fusion.1 = f32[2,64,512]{2,1,0:T(8,128)S(1)} fusion(bf16[2,512,1024]{2,1,0:T(8,128)(2,1)S(1)} %bitcast.30, f32[1024,2,64]{0,2,1:T(8,128)S(1)} %copy.20, f32[1024,2,64]{0,2,1:T(8,128)} %copy.18, f32[1024]{0:T(1024)S(1)} %sqrt_select_fusion, f32[1024]{0:T(1024)S(1)} %get-tuple-element.5), kind=kOutput, calls=%fused_computation.10 | convolution fusion | flops 134742016 | bytes 3416064 | tf_op jit(solution)/shard_map/rbk,rck->rbc/dot_general | solution.py:77
  113.3 0.0 copy-done.2
  113.3 1.1 fusion.5
  114.4 0.2 copy.23
  114.6 0.1 reshape.113
  114.7 13.9 %all_to_all.10 = bf16[32,2,512]{2,1,0:T(2,128)(2,1)S(1)} all-to-all(bf16[32,2,512]{2,1,0:T(2,128)(2,1)S(1)} %reshape.113), channel_id=1, replica_groups=mesh['ang'=8,'rad'=32] {'rad'}, dimensions={0} | all-to-all | bytes 131072 | tf_op jit(solution)/shard_map/all_to_all | solution.py:20
  128.7 0.1 reshape.114
  128.9 0.1 copy.21
  128.9 0.1 reshape.115
  129.0 13.6 %all_to_all.11 = f32[8,1,128]{2,1,0:T(1,128)S(1)} all-to-all(f32[8,1,128]{2,1,0:T(1,128)S(1)} %reshape.115), channel_id=1, replica_groups=mesh['ang'=8,'rad'=32] {'ang'}, dimensions={0} | all-to-all | bytes 8192 | tf_op jit(solution)/shard_map/all_to_all | solution.py:26
  142.7 0.5 broadcast.127
  143.2 0.7 reduce
  143.8 0.1 reshape.116
  143.9 0.6 reduce_sum.39
  (13 shorter events, 0.1 us)
Async XLA Ops:
  6.5 17.7 %copy-start = (bf16[2,512,128]{2,1,0:T(8,128)(2,1)S(1)}, bf16[2,512,128]{2,1,0:T(8,128)(2,1)}, u32[]{:S(2)}) copy-start(bf16[2,512,128]{2,1,0:T(8,128)(2,1)} %param.6) | copy-start | bytes 786436
  6.5 82.2 %all-gather.2.cloned.1.call-start = ((), (), s32[]{:S(2)}) async-start(), calls=%async_computation.2 | async-start | bytes 2359296 | tf_op jit(solution)/shard_map/all_gather | solution.py:10
  19.6 4.6 %copy-start.1 = (bf16[128,1024]{1,0:T(8,128)(2,1)S(1)}, bf16[128,1024]{1,0:T(8,128)(2,1)}, u32[]{:S(2)}) copy-start(bf16[128,1024]{1,0:T(8,128)(2,1)} %param.7) | copy-start | bytes 786436
  111.5 1.8 %copy-start.2 = (f32[2]{0:T(128)S(1)}, f32[2]{0:T(128)}, u32[]{:S(2)}) copy-start(f32[2]{0:T(128)} %param.8) | copy-start | bytes 28
Sparse Core Ops, SparseCore 0:
  10.0 78.6 all-gather.1
where the time goes:
time: 152 us; the launch traced here: 151 us
  waiting for transfers between devices  63.8 us (42%)
  local copies, waits for them, and re-layouts  34.6 us (23%)
  blocking collectives  27.6 us (18%)
  between operations  13.6 us (9%)
  other arithmetic  6.34 us (4%)
  matrix products  5.55 us (4%)
    all_gather x1, waiting for transfers between devices, over_pieces(): return lax.all_gather(array, axis).astype(jnp.float32).sum(0)  63.8 us
    all_to_all x1, blocking collectives, sent_and_summed(): lax.all_to_all(cut_along(array, dim, devices), axis, 0, 0, tiled=True)  13.9 us
    all_to_all x1, blocking collectives, sent_and_summed_2(): lax.all_to_all(tiles, axis, split_axis=0, concat_axis=0, tiled=True)  13.6 us
    gather x2, local copies, waits for them, and re-layouts, couple(): values[..., upper_col] * upper_coef + values[..., lower_col] * lower_coef  9.62 us
    gather x2, local copies, waits for them, and re-layouts, couple(): values[..., lower_col] * lower_coef  8.93 us
    gather x1, local copies, waits for them, and re-layouts, harmonic_tables(): upper_col = inverse[upper_idx]  4.53 us
    gather x1, local copies, waits for them, and re-layouts, harmonic_tables(): lower_col = inverse[lower_idx]  4.53 us
    scatter x1, local copies, waits for them, and re-layouts, harmonic_tables(): inverse = jnp.zeros((total,), jnp.int32).at[order].set(columns)  4.31 us
  transfers between devices with their start and end apart: 1, of which 1 were waited for; matrix products, arithmetic and copies ran while one was open for 11% of the time, Pallas kernels for 0%

commit v1 on v0

v1 whole, which is shorter than its diff:
```python
import functools

import jax
import jax.numpy as jnp
from jax import lax
from jax.experimental import pallas as pl
from jax.experimental.pallas import tpu as pltpu
from jax.sharding import PartitionSpec as P

LMAX = 31
MESH = pl.DeviceIdType.MESH
F32, BF16 = jnp.float32, jnp.bfloat16
NX, NY, NZ, NC, HALF = 4, 4, 8, 2, 4
ANG, RAD = 8, 32
PTS, TOTAL = 128, 1024
PIECE = PTS * ANG // RAD


def ring(d, n):
    return min(d, n - d)


OFFSETS = sorted(
    (
        (dx, dy, dz, dc)
        for dz in range(NZ)
        for dx in range(NX)
        for dy in range(NY)
        for dc in range(NC)
        if (dx, dy, dz, dc) != (0, 0, 0, 0)
    ),
    key=lambda o: -(ring(o[0], NX) + ring(o[1], NY) + ring(o[2], NZ)),
)
PEERS = [(dz, dy) for dz in range(HALF) for dy in range(NY) if (dz, dy) != (0, 0)]


def device(x, y, z, core):
    return (x * 2 + z // HALF, (z % HALF) * (NY * NC) + y * NC + core)


def piece_of(x, half, zl, y, core):
    edge = (zl == 0) | (zl == HALF - 1)
    other = jnp.where(edge, 1 - half, half)
    pair = jnp.where(edge, zl // (HALF - 1), zl - 1)
    return ((x + y) % NX) * 2 + other, pair * 2 + core


def coupling_rows(order):
    degree = jnp.zeros(order.shape, jnp.int32)
    for edge in range(1, LMAX + 1):
        degree = degree + (order >= edge * edge).astype(jnp.int32)
    m = order - degree * degree - degree
    lf, mf = degree.astype(F32), m.astype(F32)
    upper = jnp.where(degree + 1 <= LMAX, order + 2 * degree + 2, -1)
    upper_num = (lf + 1.0) * (lf + 1.0) - mf * mf
    upper_coef = jnp.sqrt(jnp.maximum(upper_num, 0.0) / ((2.0 * lf + 1.0) * (2.0 * lf + 3.0)))
    lower = jnp.where(degree - 1 >= jnp.abs(m), order - 2 * degree, -1)
    lower_num = lf * lf - mf * mf
    lower_den = jnp.maximum((2.0 * lf - 1.0) * (2.0 * lf + 1.0), 1.0)
    lower_coef = jnp.sqrt(jnp.maximum(lower_num, 0.0) / lower_den)
    return upper.astype(F32), upper_coef, lower.astype(F32), lower_coef


def turned(block):
    rows, lanes = block.shape
    row = lax.broadcasted_iota(jnp.int32, block.shape, 0)
    group = lax.broadcasted_iota(jnp.int32, block.shape, 1) // 16
    for s in (1, 2, 4):
        below = pltpu.roll(pltpu.roll(block, rows - s, 0), 16 * s, 1)
        above = pltpu.roll(pltpu.roll(block, s, 0), lanes - 16 * s, 1)
        low_row, low_group = (row & s) == 0, (group & s) == 0
        block = jnp.where(
            low_row == low_group, block, jnp.where(low_row, below, above)
        )
    return block


def kernel(
    bound_hbm, cont_hbm, ylm_hbm, weight_ref, order_ref, out_ref,
    bound, cont, ylm, ys, ncol, z_ref, mine, m_full, cont_t, sendbuf, recvbuf,
    local_sem, out_sem, a_recv, f_recv, m_recv, relay_recv, end_send, end_recv, ready,
):
    ang, rad = lax.axis_index("ang"), lax.axis_index("rad")
    x, half = ang // 2, ang % 2
    zl, y, core = rad // (NY * NC), (rad // NC) % NY, rad % NC
    z = half * HALF + zl
    me = ang * RAD + rad

    x_peers = [device((x + d) % NX, y, z, core) for d in (2, 1, 3)]
    opposite = device(x, y, (z + HALF) % NZ, core)
    twin = device(x, y, z, 1 - core)
    peers = [device(x, (y + dy) % NY, half * HALF + (zl + dz) % HALF, core) for dz, dy in PEERS]
    edge = (zl == 0) | (zl == HALF - 1)
    z_other = jnp.where(edge, NZ - 1 - z, z)
    rows_to = device((x - y + NX) % NX, y, z_other, 1 - core)
    rows_from = device((x + y) % NX, y, z_other, 1 - core)

    barrier = pltpu.get_barrier_semaphore()
    for other in (*peers, opposite, *x_peers, twin, rows_from):
        pl.semaphore_signal(barrier, inc=1, device_id=other, device_id_type=MESH)

    def send(src, dst, send_sem, recv_sem, where):
        return pltpu.make_async_remote_copy(
            src_ref=src, dst_ref=dst, send_sem=send_sem, recv_sem=recv_sem,
            device_id=where, device_id_type=MESH,
        )

    loads = [
        pltpu.make_async_copy(ylm_hbm, ylm, local_sem.at[0]),
        pltpu.make_async_copy(cont_hbm, cont, local_sem.at[1]),
        pltpu.make_async_copy(bound_hbm, bound.at[ang], local_sem.at[2]),
    ]
    for load in loads:
        load.start()
    pl.semaphore_wait(barrier, len(peers) + 6)

    to_zl = z_other % HALF
    _, quarter_to = piece_of((x - y + NX) % NX, z_other // HALF, to_zl, y, 1 - core)
    rows = send(
        ylm_hbm.at[pl.ds(pl.multiple_of(quarter_to * PIECE, PIECE), PIECE)],
        ys, out_sem.at[0], f_recv, rows_to,
    )
    rows.start()
    across = send(bound_hbm, bound.at[ang], out_sem.at[1], a_recv.at[0], opposite)
    across.start()
    along = [
        send(bound_hbm, bound.at[ang], out_sem.at[2 + i], a_recv.at[1 + i], where)
        for i, where in enumerate(x_peers)
    ]
    for copy in along:
        copy.start()
    pl.semaphore_signal(ready.at[0], inc=1, device_id=opposite, device_id_type=MESH)

    order = order_ref[...]
    upper, upper_coef, lower, lower_coef = coupling_rows(order)
    orderf = order.astype(F32)
    for s in range(TOTAL // 128):
        ncol[pl.ds(s * 128, 128)] = jnp.broadcast_to(orderf[s : s + 1], (128, 128)).T
    loads[0].wait()

    def couple(s, carry):
        here = pl.ds(pl.multiple_of(s * 128, 128), 128)
        column = ncol[here]
        blocks = []
        for t in range(TOTAL // 128):
            cut = slice(t, t + 1)
            blocks.append(
                jnp.where(
                    column == upper[cut],
                    upper_coef[cut],
                    jnp.where(column == lower[cut], lower_coef[cut], 0.0),
                ).astype(BF16)
            )
        g = jnp.concatenate(blocks, axis=1)
        z_ref[here] = lax.dot_general(
            g, ylm[...], (((1,), (1,)), ((), ())), preferred_element_type=F32
        ).astype(BF16)
        return carry

    lax.fori_loop(0, TOTAL // 128, couple, 0)
    loads[1].wait()
    shells = weight_ref.shape[0]
    count = cont.shape[0] // shells
    for r in range(shells):
        for c in range(count // 128):
            block = cont[pl.ds(r * count + c * 128, 128)].astype(F32).T
            cont_t[pl.ds(r * 128, 128), pl.ds(c * 128, 128)] = block.astype(BF16)

    rows.wait_recv()
    mine[...] = jnp.dot(ys[...], z_ref[...], preferred_element_type=F32).astype(BF16)
    cls, quarter = piece_of(x, half, zl, y, core)
    block = cls * 4 + quarter
    own = [
        send(mine, m_full.at[block], out_sem.at[8 + i], m_recv.at[i], where)
        for i, where in enumerate(peers)
    ]
    for copy in own:
        copy.start()
    n_peers = len(peers)
    relays = [send(mine, m_full.at[block], out_sem.at[8 + n_peers], relay_recv.at[0], twin)]
    relays[0].start()
    m_full[block] = mine[...]

    pl.semaphore_wait(ready.at[0], 1)
    for where in x_peers:
        pl.semaphore_signal(ready.at[1], inc=1, device_id=where, device_id_type=MESH)

    across_in = send(bound_hbm, bound.at[ang], out_sem.at[1], a_recv.at[0], opposite)
    across_in.wait_recv()
    opposite_cls = opposite[0]
    onward = [
        send(bound.at[opposite_cls], bound.at[opposite_cls], out_sem.at[5 + i], a_recv.at[4 + i], where)
        for i, where in enumerate(x_peers)
    ]
    for copy in onward:
        copy.start()
    pl.semaphore_wait(ready.at[1], NX - 1)
    pl.semaphore_signal(ready.at[2], inc=1, device_id=twin, device_id_type=MESH)

    for i, (dz, dy) in enumerate(PEERS):
        own[i].wait_recv()
        there_cls, there_quarter = piece_of(
            x, half, (zl - dz + HALF) % HALF, (y - dy + NY) % NY, core
        )
        there = there_cls * 4 + there_quarter
        relay = send(
            m_full.at[there], m_full.at[there],
            out_sem.at[9 + n_peers + i], relay_recv.at[1 + i], twin,
        )
        relay.start()
        relays.append(relay)
    loads[2].wait()
    for copy in along:
        copy.wait_recv()
    for copy in onward:
        copy.wait_recv()
    bound_all = jnp.concatenate([bound[i] for i in range(ANG)], axis=1)
    pl.semaphore_wait(ready.at[2], 1)
    for relay in relays:
        relay.wait_recv()

    operator = m_full[...].reshape(PTS * ANG, PTS)
    d = jnp.dot(bound_all, operator, preferred_element_type=F32)
    nb = d.shape[0] // shells
    weighted = [d[r * nb : (r + 1) * nb] * weight_ref[r] for r in range(shells)]
    wide = jnp.concatenate(weighted, axis=1).astype(BF16)
    terms = jnp.dot(wide, cont_t[...], preferred_element_type=F32)
    for q in range(count // 128):
        cut = turned(terms[:, q * 128 : (q + 1) * 128])
        for a in range(ANG):
            sendbuf[pl.ds(a * RAD + q * 8, 8)] = cut[a * 8 : a * 8 + 8]

    for dx, dy, dz, dc in OFFSETS:
        where = device((x + dx) % NX, (y + dy) % NY, (z + dz) % NZ, (core + dc) % NC)
        send(
            sendbuf.at[pl.ds(where[0] * RAD + where[1], 1)],
            recvbuf.at[pl.ds(me, 1)],
            end_send, end_recv, where,
        ).start()
    pltpu.make_async_copy(
        sendbuf.at[pl.ds(me, 1)], recvbuf.at[pl.ds(me, 1)], end_recv
    ).start()
    for copy in (rows, across, *along, *onward, *own, *relays):
        copy.wait_send()
    pltpu.make_async_copy(sendbuf, recvbuf, end_recv).wait()
    row = jnp.sum(recvbuf[...], axis=0, keepdims=True)
    wide_row = jnp.broadcast_to(row, (8, 128))
    at = lax.broadcasted_iota(jnp.int32, (8, 128), 0)
    spread = wide_row
    for j in range(1, 8):
        spread = jnp.where(at == j, pltpu.roll(wide_row, 128 - 16 * j, 1), spread)
    out_ref[...] = spread[:, : out_ref.shape[1]]
    pltpu.make_async_copy(
        sendbuf.at[pl.ds(0, ANG * RAD - 1)], recvbuf.at[pl.ds(0, ANG * RAD - 1)], end_send
    ).wait()


def shards(psi_bound, psi_cont, ylm, radial_weight, order):
    shells, nb, points = psi_bound.shape
    count = psi_cont.shape[1]
    any_space = pl.BlockSpec(memory_space=pl.ANY)
    dma = pltpu.SemaphoreType.DMA
    n_peers = len(PEERS)
    return pl.pallas_call(
        kernel,
        out_shape=jax.ShapeDtypeStruct((nb // ANG, count // RAD), F32),
        in_specs=[
            any_space,
            any_space,
            any_space,
            pl.BlockSpec(memory_space=pltpu.SMEM),
            pl.BlockSpec(memory_space=pltpu.VMEM),
        ],
        out_specs=pl.BlockSpec(memory_space=pltpu.VMEM),
        scratch_shapes=[
            pltpu.VMEM((ANG, shells * nb, points), BF16),
            pltpu.VMEM((shells * count, points), BF16),
            pltpu.VMEM((points, TOTAL), BF16),
            pltpu.VMEM((PIECE, TOTAL), BF16),
            pltpu.VMEM((TOTAL, 128), F32),
            pltpu.VMEM((TOTAL, points), BF16),
            pltpu.VMEM((PIECE, points), BF16),
            pltpu.VMEM((RAD, PIECE, points), BF16),
            pltpu.VMEM((shells * points, count), BF16),
            pltpu.VMEM((ANG * RAD, 128), F32),
            pltpu.VMEM((ANG * RAD, 128), F32),
            dma((3,)),
            dma((9 + 2 * n_peers,)),
            dma((7,)),
            dma,
            dma((n_peers,)),
            dma((n_peers + 1,)),
            dma,
            dma,
            pltpu.SemaphoreType.REGULAR((3,)),
        ],
        compiler_params=pltpu.CompilerParams(collective_id=0, has_side_effects=True),
        name="dipole",
    )(
        psi_bound.reshape(shells * nb, points),
        psi_cont.reshape(shells * count, points),
        ylm,
        radial_weight,
        order.reshape(8, TOTAL // 8),
    )


def solution(mesh):
    return jax.shard_map(
        shards,
        mesh=mesh,
        in_specs=(P("rad", None, "ang"), P("rad", None, "ang"), P("ang", None), P("rad"), P()),
        out_specs=P("ang", "rad"),
        check_vma=False,
    )
```

time: 152 us -> 34.4 us (0.23)
  waiting for transfers between devices: 63.8 us -> 0 us
  local copies, waits for them, and re-layouts: 34.6 us -> 1.28 us
  Pallas kernels: 0 us -> 33 us
  blocking collectives: 27.6 us -> 0 us
  between operations: 13.6 us -> 0.01 us
  other arithmetic: 6.34 us -> 0 us
  matrix products: 5.55 us -> 0 us
    all_gather x1 -> x0, waiting for transfers between devices: 63.8 us -> none  [over_pieces(): return lax.all_gather(array, axis).astype(jnp.float32).sum(0)]
    pallas_call x0 -> x1, Pallas kernels: none -> 33 us  [shards(): pl.pallas_call(kernel, out_shape=jax.ShapeDtypeStruct((nb // ANG, count /...]
    gather x6 -> x0, local copies, waits for them, and re-layouts: 27.6 us -> none  [the longest x2 9.62 us: couple(): values[..., upper_col] * upper_coef + values[..., lower_col] * lower_coef]
    all_to_all x2 -> x0, blocking collectives: 27.6 us -> none  [the longest x1 13.9 us: sent_and_summed(): lax.all_to_all(cut_along(array, dim, devices), axis, 0, 0, tiled=True)]
    dot_general x4 -> x0, matrix products: 5.55 us -> none  [the longest x1 1.95 us: shards(): jnp.dot(psi_bound.reshape(shells * bound_count, points), ylm, preferred_e...]
    scatter x1 -> x0, local copies, waits for them, and re-layouts: 4.31 us -> none  [harmonic_tables(): inverse = jnp.zeros((total,), jnp.int32).at[order].set(columns)]
    reduce_sum x4 -> x0, other arithmetic: 4.23 us -> none  [the longest x1 2.79 us: over_pieces(): return lax.all_gather(array, axis).astype(jnp.float32).sum(0)]
    reduce_sum x2 -> x0, local copies, waits for them, and re-layouts: 1.53 us -> none  [the longest x1 1.45 us: over_pieces(): return lax.all_gather(array, axis).astype(jnp.float32).sum(0)]
  transfers between devices with their start and end apart: 1 -> 0, of which waited for: 1 -> 0; matrix products, arithmetic and copies ran while one was open for 11% -> 0% of each run, Pallas kernels for 0% -> 0%
where the time goes in v1:
time: 34.4 us; the launch traced here: 34.2 us
  Pallas kernels  33 us (96%)
  local copies, waits for them, and re-layouts  1.28 us (4%)
    pallas_call x1, Pallas kernels, shards(): pl.pallas_call(kernel, out_shape=jax.ShapeDtypeStruct((nb // ANG, count /...  33 us
    unnamed x1, local copies, waits for them, and re-layouts  1.28 us

profile of v1, /device:TPU:1, one launch (start us, length us, event | category | flops | bytes accessed | tf_op | source)
XLA Modules:
  0.0 34.2 jit_solution(15751482879130715451)
XLA Ops:
  0.0 33.0 %dipole.1 = f32[8,16]{1,0:T(8,128)} custom-call(bf16[128,128]{1,0:T(8,128)(2,1)} %bitcast.4, bf16[1024,128]{1,0:T(8,128)(2,1)} %bitcast.3, bf16[128,1024]{1,0:T(8,128)(2,1)} %ylm_hbm.1, f32[2]{0:T(128)} %weight_ref.1, s32[8,128]{1,0:T(8,128)} %bitcast.5), custom_call_target="tpu_custom_call" | custom-call | tf_op jit(solution)/shard_map/dipole/pallas_call | solution.py:264
  33.0 1.3 %copy.7 = f32[8,16]{1,0:T(8,128)} copy(f32[8,16]{1,0:T(8,128)} %dipole.1) | data formatting | bytes 1024

commit v2 on v1

--- a/solution.py
+++ b/solution.py
@@ -8,7 +8,6 @@
 from jax.sharding import PartitionSpec as P
 
 LMAX = 31
-MESH = pl.DeviceIdType.MESH
 F32, BF16 = jnp.float32, jnp.bfloat16
 NX, NY, NZ, NC, HALF = 4, 4, 8, 2, 4
 ANG, RAD = 8, 32
@@ -20,29 +19,29 @@
     return min(d, n - d)
 
 
-OFFSETS = sorted(
-    (
-        (dx, dy, dz, dc)
-        for dz in range(NZ)
-        for dx in range(NX)
-        for dy in range(NY)
-        for dc in range(NC)
-        if (dx, dy, dz, dc) != (0, 0, 0, 0)
-    ),
-    key=lambda o: -(ring(o[0], NX) + ring(o[1], NY) + ring(o[2], NZ)),
+PLANE = sorted(
+    ((dx, dy, dc) for dx in range(NX) for dy in range(NY) for dc in range(NC) if (dx, dy, dc) != (0, 0, 0)),
+    key=lambda o: -(ring(o[0], NX) + ring(o[1], NY)),
 )
 PEERS = [(dz, dy) for dz in range(HALF) for dy in range(NY) if (dz, dy) != (0, 0)]
-
-
-def device(x, y, z, core):
-    return (x * 2 + z // HALF, (z % HALF) * (NY * NC) + y * NC + core)
+BY_ID = pl.DeviceIdType.LOGICAL
+
+
+def device(place):
+    x, y, z, core = place
+    return x * (ANG * RAD // NX) + z * (NY * NC) + y * NC + core
+
+
+def turn_of(place):
+    x, y, z, core = place
+    return z * 32 + y * 8 + x * 2 + (1 - core)
 
 
 def piece_of(x, half, zl, y, core):
     edge = (zl == 0) | (zl == HALF - 1)
     other = jnp.where(edge, 1 - half, half)
     pair = jnp.where(edge, zl // (HALF - 1), zl - 1)
-    return ((x + y) % NX) * 2 + other, pair * 2 + core
+    return ((x - y + 2 + NX) % NX) * 2 + other, pair * 2 + core
 
 
 def coupling_rows(order):
@@ -76,9 +75,9 @@
 
 
 def kernel(
-    bound_hbm, cont_hbm, ylm_hbm, weight_ref, order_ref, out_ref,
-    bound, cont, ylm, ys, ncol, z_ref, mine, m_full, cont_t, sendbuf, recvbuf,
-    local_sem, out_sem, a_recv, f_recv, m_recv, relay_recv, end_send, end_recv, ready,
+    bound_hbm, cont_hbm, ylm_hbm, weight_hbm, order_hbm, out_ref,
+    bound, cont, ylm, order_ref, weight_ref, ys, ncol, z_ref, mine, m_full, cont_t, sendbuf, recvbuf,
+    local_sem, out_sem, a_recv, f_recv, m_recv, relay_recv, end_send, end_recv, here, all_here,
 ):
     ang, rad = lax.axis_index("ang"), lax.axis_index("rad")
     x, half = ang // 2, ang % 2
@@ -86,57 +85,91 @@
     z = half * HALF + zl
     me = ang * RAD + rad
 
-    x_peers = [device((x + d) % NX, y, z, core) for d in (2, 1, 3)]
-    opposite = device(x, y, (z + HALF) % NZ, core)
-    twin = device(x, y, z, 1 - core)
-    peers = [device(x, (y + dy) % NY, half * HALF + (zl + dz) % HALF, core) for dz, dy in PEERS]
+    x_peers = [((x + d) % NX, y, z, core) for d in (2, 1, 3)]
+    opposite = (x, y, (z + HALF) % NZ, core)
+    twin = (x, y, z, 1 - core)
+    peers = [(x, (y + dy) % NY, half * HALF + (zl + dz) % HALF, core) for dz, dy in PEERS]
     edge = (zl == 0) | (zl == HALF - 1)
     z_other = jnp.where(edge, NZ - 1 - z, z)
-    rows_to = device((x - y + NX) % NX, y, z_other, 1 - core)
-    rows_from = device((x + y) % NX, y, z_other, 1 - core)
-
+    rows_to = ((x + y + 2) % NX, y, z_other, 1 - core)
+    rows_from = ((x - y + 2 + NX) % NX, y, z_other, 1 - core)
+
+    turn = turn_of((x, y, z, core))
+    links = [(rows_from, 2), (opposite, 1), *((p, 0) for p in x_peers), *((p, 3) for p in peers), (twin, 3), (rows_to, None)]
+    firsts = [turn < turn_of(place) for place, _ in links]
     barrier = pltpu.get_barrier_semaphore()
-    for other in (*peers, opposite, *x_peers, twin, rows_from):
-        pl.semaphore_signal(barrier, inc=1, device_id=other, device_id_type=MESH)
+    before = 0
+    for (place, _), first in zip(links, firsts):
+        before = before + jnp.where(first, 0, 1)
+
+        @pl.when(first)
+        def _():
+            pl.semaphore_signal(barrier, inc=1, device_id=device(place), device_id_type=BY_ID)
 
     def send(src, dst, send_sem, recv_sem, where):
         return pltpu.make_async_remote_copy(
             src_ref=src, dst_ref=dst, send_sem=send_sem, recv_sem=recv_sem,
-            device_id=where, device_id_type=MESH,
+            device_id=device(where), device_id_type=BY_ID,
         )
 
     loads = [
+        pltpu.make_async_copy(order_hbm, order_ref, local_sem.at[3]),
         pltpu.make_async_copy(ylm_hbm, ylm, local_sem.at[0]),
         pltpu.make_async_copy(cont_hbm, cont, local_sem.at[1]),
         pltpu.make_async_copy(bound_hbm, bound.at[ang], local_sem.at[2]),
-    ]
+        pltpu.make_async_copy(weight_hbm, weight_ref, local_sem.at[4]),
+    ]
+    load_order, load_ylm, load_cont, load_bound, load_weight = loads
     for load in loads:
         load.start()
-    pl.semaphore_wait(barrier, len(peers) + 6)
-
-    to_zl = z_other % HALF
-    _, quarter_to = piece_of((x - y + NX) % NX, z_other // HALF, to_zl, y, 1 - core)
+
+    @pl.when(before > 0)
+    def _():
+        pl.semaphore_wait(barrier, before)
+
+    for (place, kind), first in zip(links, firsts):
+        if kind is not None:
+
+            @pl.when(jnp.logical_not(first))
+            def _():
+                pl.semaphore_signal(here.at[kind], inc=1, device_id=device(place), device_id_type=BY_ID)
+
+    _, quarter_to = piece_of(rows_to[0], z_other // HALF, z_other % HALF, y, 1 - core)
     rows = send(
         ylm_hbm.at[pl.ds(pl.multiple_of(quarter_to * PIECE, PIECE), PIECE)],
         ys, out_sem.at[0], f_recv, rows_to,
     )
-    rows.start()
     across = send(bound_hbm, bound.at[ang], out_sem.at[1], a_recv.at[0], opposite)
-    across.start()
     along = [
         send(bound_hbm, bound.at[ang], out_sem.at[2 + i], a_recv.at[1 + i], where)
         for i, where in enumerate(x_peers)
     ]
+
+    def wait_for(kind, *which):
+        count = sum(jnp.where(firsts[i], 1, 0) for i in which)
+
+        @pl.when(count > 0)
+        def _():
+            pl.semaphore_wait(here.at[kind], count)
+
+    wait_for(2, len(links) - 1)
+    rows.start()
+    wait_for(0, 2, 3, 4)
     for copy in along:
         copy.start()
-    pl.semaphore_signal(ready.at[0], inc=1, device_id=opposite, device_id_type=MESH)
-
+
+
+    @pl.when(jnp.logical_not(firsts[1]))
+    def _():
+        across.start()
+
+    load_order.wait()
     order = order_ref[...]
     upper, upper_coef, lower, lower_coef = coupling_rows(order)
     orderf = order.astype(F32)
     for s in range(TOTAL // 128):
         ncol[pl.ds(s * 128, 128)] = jnp.broadcast_to(orderf[s : s + 1], (128, 128)).T
-    loads[0].wait()
+    load_ylm.wait()
 
     def couple(s, carry):
         here = pl.ds(pl.multiple_of(s * 128, 128), 128)
@@ -158,7 +191,13 @@
         return carry
 
     lax.fori_loop(0, TOTAL // 128, couple, 0)
-    loads[1].wait()
+
+    @pl.when(firsts[1])
+    def _():
+        pl.semaphore_wait(here.at[1], 1)
+        across.start()
+
+    load_cont.wait()
     shells = weight_ref.shape[0]
     count = cont.shape[0] // shells
     for r in range(shells):
@@ -170,6 +209,7 @@
     mine[...] = jnp.dot(ys[...], z_ref[...], preferred_element_type=F32).astype(BF16)
     cls, quarter = piece_of(x, half, zl, y, core)
     block = cls * 4 + quarter
+    wait_for(3, *range(5, 6 + len(peers)))
     own = [
         send(mine, m_full.at[block], out_sem.at[8 + i], m_recv.at[i], where)
         for i, where in enumerate(peers)
@@ -181,21 +221,18 @@
     relays[0].start()
     m_full[block] = mine[...]
 
-    pl.semaphore_wait(ready.at[0], 1)
-    for where in x_peers:
-        pl.semaphore_signal(ready.at[1], inc=1, device_id=where, device_id_type=MESH)
-
-    across_in = send(bound_hbm, bound.at[ang], out_sem.at[1], a_recv.at[0], opposite)
-    across_in.wait_recv()
-    opposite_cls = opposite[0]
+    pl.semaphore_signal(all_here.at[0], inc=1, device_id=device(opposite), device_id_type=BY_ID)
+    across.wait_recv()
+    opposite_cls = x * 2 + 1 - half
     onward = [
         send(bound.at[opposite_cls], bound.at[opposite_cls], out_sem.at[5 + i], a_recv.at[4 + i], where)
         for i, where in enumerate(x_peers)
     ]
     for copy in onward:
         copy.start()
-    pl.semaphore_wait(ready.at[1], NX - 1)
-    pl.semaphore_signal(ready.at[2], inc=1, device_id=twin, device_id_type=MESH)
+    pl.semaphore_wait(all_here.at[0], 1)
+    for where in x_peers:
+        pl.semaphore_signal(all_here.at[1], inc=1, device_id=device(where), device_id_type=BY_ID)
 
     for i, (dz, dy) in enumerate(PEERS):
         own[i].wait_recv()
@@ -209,15 +246,16 @@
         )
         relay.start()
         relays.append(relay)
-    loads[2].wait()
-    for copy in along:
+    load_bound.wait()
+    load_weight.wait()
+    for copy in (*along, *onward):
         copy.wait_recv()
-    for copy in onward:
-        copy.wait_recv()
+    pl.semaphore_wait(all_here.at[1], NX - 1)
+    pl.semaphore_signal(all_here.at[2], inc=1, device_id=device(twin), device_id_type=BY_ID)
     bound_all = jnp.concatenate([bound[i] for i in range(ANG)], axis=1)
-    pl.semaphore_wait(ready.at[2], 1)
     for relay in relays:
         relay.wait_recv()
+    pl.semaphore_wait(all_here.at[2], 1)
 
     operator = m_full[...].reshape(PTS * ANG, PTS)
     d = jnp.dot(bound_all, operator, preferred_element_type=F32)
@@ -230,13 +268,21 @@
         for a in range(ANG):
             sendbuf[pl.ds(a * RAD + q * 8, 8)] = cut[a * 8 : a * 8 + 8]
 
-    for dx, dy, dz, dc in OFFSETS:
-        where = device((x + dx) % NX, (y + dy) % NY, (z + dz) % NZ, (core + dc) % NC)
-        send(
-            sendbuf.at[pl.ds(where[0] * RAD + where[1], 1)],
-            recvbuf.at[pl.ds(me, 1)],
-            end_send, end_recv, where,
+    def give(number):
+        pltpu.make_async_remote_copy(
+            src_ref=sendbuf.at[pl.ds(number, 1)], dst_ref=recvbuf.at[pl.ds(me, 1)],
+            send_sem=end_send, recv_sem=end_recv, device_id=number, device_id_type=BY_ID,
         ).start()
+
+    columns = [
+        device(((x + dx) % NX, (y + dy) % NY, 0, (core + dc) % NC)) for dx, dy, dc in PLANE
+    ]
+    for zs in (range(HALF), range(HALF, NZ)):
+        for column in columns:
+            for there in zs:
+                give(column + there * (NY * NC))
+    for dz in (4, 3, 5, 2, 6, 1, 7):
+        give(device((x, y, (z + dz) % NZ, core)))
     pltpu.make_async_copy(
         sendbuf.at[pl.ds(me, 1)], recvbuf.at[pl.ds(me, 1)], end_recv
     ).start()
@@ -268,14 +314,16 @@
             any_space,
             any_space,
             any_space,
-            pl.BlockSpec(memory_space=pltpu.SMEM),
-            pl.BlockSpec(memory_space=pltpu.VMEM),
+            any_space,
+            any_space,
         ],
         out_specs=pl.BlockSpec(memory_space=pltpu.VMEM),
         scratch_shapes=[
             pltpu.VMEM((ANG, shells * nb, points), BF16),
             pltpu.VMEM((shells * count, points), BF16),
             pltpu.VMEM((points, TOTAL), BF16),
+            pltpu.VMEM((8, TOTAL // 8), jnp.int32),
+            pltpu.SMEM((shells,), F32),
             pltpu.VMEM((PIECE, TOTAL), BF16),
             pltpu.VMEM((TOTAL, 128), F32),
             pltpu.VMEM((TOTAL, points), BF16),
@@ -284,7 +332,7 @@
             pltpu.VMEM((shells * points, count), BF16),
             pltpu.VMEM((ANG * RAD, 128), F32),
             pltpu.VMEM((ANG * RAD, 128), F32),
-            dma((3,)),
+            dma((5,)),
             dma((9 + 2 * n_peers,)),
             dma((7,)),
             dma,
@@ -292,6 +340,7 @@
             dma((n_peers + 1,)),
             dma,
             dma,
+            pltpu.SemaphoreType.REGULAR((4,)),
             pltpu.SemaphoreType.REGULAR((3,)),
         ],
         compiler_params=pltpu.CompilerParams(collective_id=0, has_side_effects=True),

time: 34.4 us -> 35.9 us (1.044)
  Pallas kernels: 33 us -> 34.5 us
    pallas_call x1, Pallas kernels: 33 us -> 34.5 us  [shards(): pl.pallas_call(kernel, out_shape=jax.ShapeDtypeStruct((nb // ANG, count /...]
where the time goes in v2:
time: 35.9 us; the launch traced here: 35.7 us
  Pallas kernels  34.5 us (96%)
  local copies, waits for them, and re-layouts  1.28 us (4%)
    pallas_call x1, Pallas kernels, shards(): pl.pallas_call(kernel, out_shape=jax.ShapeDtypeStruct((nb // ANG, count /...  34.5 us
    unnamed x1, local copies, waits for them, and re-layouts  1.28 us

profile of v2, /device:TPU:1, one launch (start us, length us, event | category | flops | bytes accessed | tf_op | source)
XLA Modules:
  0.0 35.7 jit_solution(12408862958125320799)
XLA Ops:
  0.0 34.5 %dipole.1 = f32[8,16]{1,0:T(8,128)} custom-call(bf16[128,128]{1,0:T(8,128)(2,1)} %bitcast.4, bf16[1024,128]{1,0:T(8,128)(2,1)} %bitcast.3, bf16[128,1024]{1,0:T(8,128)(2,1)} %ylm_hbm.1, f32[2]{0:T(128)} %weight_hbm.1, s32[8,128]{1,0:T(8,128)} %bitcast.5), custom_call_target="tpu_custom_call" | custom-call | tf_op jit(solution)/shard_map/dipole/pallas_call | solution.py:310
  34.5 1.3 %copy.7 = f32[8,16]{1,0:T(8,128)} copy(f32[8,16]{1,0:T(8,128)} %dipole.1) | data formatting | bytes 1024

commit v3 on v2

--- a/solution.py
+++ b/solution.py
@@ -23,7 +23,6 @@
     ((dx, dy, dc) for dx in range(NX) for dy in range(NY) for dc in range(NC) if (dx, dy, dc) != (0, 0, 0)),
     key=lambda o: -(ring(o[0], NX) + ring(o[1], NY)),
 )
-PEERS = [(dz, dy) for dz in range(HALF) for dy in range(NY) if (dz, dy) != (0, 0)]
 BY_ID = pl.DeviceIdType.LOGICAL
 
 
@@ -40,8 +39,8 @@
 def piece_of(x, half, zl, y, core):
     edge = (zl == 0) | (zl == HALF - 1)
     other = jnp.where(edge, 1 - half, half)
-    pair = jnp.where(edge, zl // (HALF - 1), zl - 1)
-    return ((x - y + 2 + NX) % NX) * 2 + other, pair * 2 + core
+    pair = jnp.where(edge, lax.div(zl, HALF - 1), zl - 1)
+    return lax.rem(x - y + 2 + NX, NX) * 2 + other, pair * 2 + core
 
 
 def coupling_rows(order):
@@ -80,88 +79,119 @@
     local_sem, out_sem, a_recv, f_recv, m_recv, relay_recv, end_send, end_recv, here, all_here,
 ):
     ang, rad = lax.axis_index("ang"), lax.axis_index("rad")
-    x, half = ang // 2, ang % 2
-    zl, y, core = rad // (NY * NC), (rad // NC) % NY, rad % NC
+    x, half, core, spot = lax.div(ang, 2), lax.rem(ang, 2), lax.rem(rad, NC), lax.div(rad, NC)
+    zl, y = lax.div(spot, NY), lax.rem(spot, NY)
     z = half * HALF + zl
     me = ang * RAD + rad
-
-    x_peers = [((x + d) % NX, y, z, core) for d in (2, 1, 3)]
-    opposite = (x, y, (z + HALF) % NZ, core)
-    twin = (x, y, z, 1 - core)
-    peers = [(x, (y + dy) % NY, half * HALF + (zl + dz) % HALF, core) for dz, dy in PEERS]
+    x_step = ANG * RAD // NX
+    x_peers = [me + (lax.rem(x + d, NX) - x) * x_step for d in (2, 1, 3)]
+    opposite = me + RAD - 2 * RAD * half
+    twin = me + 1 - 2 * core
+    first_spot = me - NC * spot
     edge = (zl == 0) | (zl == HALF - 1)
     z_other = jnp.where(edge, NZ - 1 - z, z)
-    rows_to = ((x + y + 2) % NX, y, z_other, 1 - core)
-    rows_from = ((x - y + 2 + NX) % NX, y, z_other, 1 - core)
-
     turn = turn_of((x, y, z, core))
-    links = [(rows_from, 2), (opposite, 1), *((p, 0) for p in x_peers), *((p, 3) for p in peers), (twin, 3), (rows_to, None)]
-    firsts = [turn < turn_of(place) for place, _ in links]
-    barrier = pltpu.get_barrier_semaphore()
-    before = 0
-    for (place, _), first in zip(links, firsts):
-        before = before + jnp.where(first, 0, 1)
-
-        @pl.when(first)
-        def _():
-            pl.semaphore_signal(barrier, inc=1, device_id=device(place), device_id_type=BY_ID)
+    to_x, from_x = lax.rem(x + y + 2, NX), lax.rem(x - y + 2 + NX, NX)
+    rows_to, rows_from = (device((i, y, z_other, 1 - core)) for i in (to_x, from_x))
+    ahead_to, ahead_from = (turn < turn_of((i, y, z_other, 1 - core)) for i in (to_x, from_x))
+    count = lambda flag: jnp.where(flag, 1, 0)
+
+    def signal(semaphore, where):
+        pl.semaphore_signal(semaphore, inc=1, device_id=where, device_id_type=BY_ID)
+
+    def each(start, end, act):
+        def body(i, carry):
+            act(i)
+            return carry
+
+        lax.fori_loop(start, end, body, 0)
 
     def send(src, dst, send_sem, recv_sem, where):
         return pltpu.make_async_remote_copy(
             src_ref=src, dst_ref=dst, send_sem=send_sem, recv_sem=recv_sem,
-            device_id=device(where), device_id_type=BY_ID,
+            device_id=where, device_id_type=BY_ID,
         )
 
     loads = [
+        pltpu.make_async_copy(ylm_hbm, ylm, local_sem.at[0]),
         pltpu.make_async_copy(order_hbm, order_ref, local_sem.at[3]),
-        pltpu.make_async_copy(ylm_hbm, ylm, local_sem.at[0]),
         pltpu.make_async_copy(cont_hbm, cont, local_sem.at[1]),
         pltpu.make_async_copy(bound_hbm, bound.at[ang], local_sem.at[2]),
         pltpu.make_async_copy(weight_hbm, weight_ref, local_sem.at[4]),
     ]
-    load_order, load_ylm, load_cont, load_bound, load_weight = loads
+    load_ylm, load_order, load_cont, load_bound, load_weight = loads
     for load in loads:
         load.start()
 
+    barrier = pltpu.get_barrier_semaphore()
+
+    @pl.when(ahead_from)
+    def _():
+        signal(barrier, rows_from)
+
+    @pl.when(ahead_to)
+    def _():
+        signal(barrier, rows_to)
+
+    @pl.when(half == 0)
+    def _():
+        signal(barrier, opposite)
+
+    each(x + 1, NX, lambda i: signal(barrier, me + (i - x) * x_step))
+
+    @pl.when(core == 1)
+    def _():
+        signal(barrier, twin)
+
+    each(spot + 1, RAD // NC, lambda i: signal(barrier, first_spot + NC * i))
+    before = 2 - count(ahead_from) - count(ahead_to) + half + x + (1 - core) + spot
+
     @pl.when(before > 0)
     def _():
         pl.semaphore_wait(barrier, before)
 
-    for (place, kind), first in zip(links, firsts):
-        if kind is not None:
-
-            @pl.when(jnp.logical_not(first))
-            def _():
-                pl.semaphore_signal(here.at[kind], inc=1, device_id=device(place), device_id_type=BY_ID)
-
-    _, quarter_to = piece_of(rows_to[0], z_other // HALF, z_other % HALF, y, 1 - core)
+    @pl.when(jnp.logical_not(ahead_from))
+    def _():
+        signal(here.at[2], rows_from)
+
+    quarter_to = piece_of(to_x, lax.div(z_other, HALF), lax.rem(z_other, HALF), y, 1 - core)[1]
     rows = send(
         ylm_hbm.at[pl.ds(pl.multiple_of(quarter_to * PIECE, PIECE), PIECE)],
         ys, out_sem.at[0], f_recv, rows_to,
     )
     across = send(bound_hbm, bound.at[ang], out_sem.at[1], a_recv.at[0], opposite)
+
+    @pl.when(jnp.logical_not(ahead_to))
+    def _():
+        rows.start()
+
+    each(0, x, lambda i: signal(here.at[0], me + (i - x) * x_step))
+
+    @pl.when(half == 1)
+    def _():
+        signal(here.at[1], opposite)
+        across.start()
+
+    @pl.when(core == 0)
+    def _():
+        signal(here.at[3], twin)
+
+    each(0, spot, lambda i: signal(here.at[3], first_spot + NC * i))
+
+    @pl.when(ahead_to)
+    def _():
+        pl.semaphore_wait(here.at[2], 1)
+        rows.start()
+
+    @pl.when(x < NX - 1)
+    def _():
+        pl.semaphore_wait(here.at[0], NX - 1 - x)
+
     along = [
-        send(bound_hbm, bound.at[ang], out_sem.at[2 + i], a_recv.at[1 + i], where)
-        for i, where in enumerate(x_peers)
+        send(bound_hbm, bound.at[ang], out_sem.at[2], a_recv.at[1], where) for where in x_peers
     ]
-
-    def wait_for(kind, *which):
-        count = sum(jnp.where(firsts[i], 1, 0) for i in which)
-
-        @pl.when(count > 0)
-        def _():
-            pl.semaphore_wait(here.at[kind], count)
-
-    wait_for(2, len(links) - 1)
-    rows.start()
-    wait_for(0, 2, 3, 4)
     for copy in along:
         copy.start()
-
-
-    @pl.when(jnp.logical_not(firsts[1]))
-    def _():
-        across.start()
 
     load_order.wait()
     order = order_ref[...]
@@ -192,69 +222,68 @@
 
     lax.fori_loop(0, TOTAL // 128, couple, 0)
 
-    @pl.when(firsts[1])
+    @pl.when(half == 0)
     def _():
         pl.semaphore_wait(here.at[1], 1)
         across.start()
 
-    load_cont.wait()
-    shells = weight_ref.shape[0]
-    count = cont.shape[0] // shells
-    for r in range(shells):
-        for c in range(count // 128):
-            block = cont[pl.ds(r * count + c * 128, 128)].astype(F32).T
-            cont_t[pl.ds(r * 128, 128), pl.ds(c * 128, 128)] = block.astype(BF16)
-
+    def block_of(i):
+        cls, quarter = piece_of(x, half, lax.div(i, NY), lax.rem(i, NY), core)
+        return cls * (RAD // ANG) + quarter
+
+    block = block_of(spot)
     rows.wait_recv()
     mine[...] = jnp.dot(ys[...], z_ref[...], preferred_element_type=F32).astype(BF16)
-    cls, quarter = piece_of(x, half, zl, y, core)
-    block = cls * 4 + quarter
-    wait_for(3, *range(5, 6 + len(peers)))
-    own = [
-        send(mine, m_full.at[block], out_sem.at[8 + i], m_recv.at[i], where)
-        for i, where in enumerate(peers)
-    ]
-    for copy in own:
-        copy.start()
-    n_peers = len(peers)
-    relays = [send(mine, m_full.at[block], out_sem.at[8 + n_peers], relay_recv.at[0], twin)]
-    relays[0].start()
+    spots = RAD // NC
+    later_ones = spots - 1 - spot + core
+
+    @pl.when(later_ones > 0)
+    def _():
+        pl.semaphore_wait(here.at[3], later_ones)
+
+    def give_piece(i):
+        send(mine, m_full.at[block], out_sem.at[3], m_recv.at[spot], first_spot + NC * i).start()
+
+    each(spot + 1, spots, give_piece)
+    each(0, spot, give_piece)
+    send(mine, m_full.at[block], out_sem.at[4], relay_recv, twin).start()
     m_full[block] = mine[...]
 
-    pl.semaphore_signal(all_here.at[0], inc=1, device_id=device(opposite), device_id_type=BY_ID)
+    signal(all_here.at[0], opposite)
     across.wait_recv()
-    opposite_cls = x * 2 + 1 - half
-    onward = [
-        send(bound.at[opposite_cls], bound.at[opposite_cls], out_sem.at[5 + i], a_recv.at[4 + i], where)
-        for i, where in enumerate(x_peers)
-    ]
+    other_cls = bound.at[ang + 1 - 2 * half]
+    onward = [send(other_cls, other_cls, out_sem.at[5], a_recv.at[2], where) for where in x_peers]
     for copy in onward:
         copy.start()
     pl.semaphore_wait(all_here.at[0], 1)
     for where in x_peers:
-        pl.semaphore_signal(all_here.at[1], inc=1, device_id=device(where), device_id_type=BY_ID)
-
-    for i, (dz, dy) in enumerate(PEERS):
-        own[i].wait_recv()
-        there_cls, there_quarter = piece_of(
-            x, half, (zl - dz + HALF) % HALF, (y - dy + NY) % NY, core
-        )
-        there = there_cls * 4 + there_quarter
-        relay = send(
-            m_full.at[there], m_full.at[there],
-            out_sem.at[9 + n_peers + i], relay_recv.at[1 + i], twin,
-        )
-        relay.start()
-        relays.append(relay)
+        signal(all_here.at[1], where)
+
+    load_cont.wait()
+    shells = weight_ref.shape[0]
+    count_c = cont.shape[0] // shells
+    for r in range(shells):
+        for c in range(count_c // 128):
+            part = cont[pl.ds(r * count_c + c * 128, 128)].astype(F32).T
+            cont_t[pl.ds(r * 128, 128), pl.ds(c * 128, 128)] = part.astype(BF16)
+
+    def pass_on(i):
+        there = m_full.at[block_of(i)]
+        send(there, there, out_sem.at[4], m_recv.at[i], twin).wait_recv()
+        send(there, there, out_sem.at[4], relay_recv, twin).start()
+
+    each(0, spot, pass_on)
+    each(spot + 1, spots, pass_on)
     load_bound.wait()
     load_weight.wait()
-    for copy in (*along, *onward):
-        copy.wait_recv()
+    three = bound.at[pl.ds(0, NX - 1)]
+    for i in (1, 2):
+        send(three, three, out_sem.at[2], a_recv.at[i], twin).wait_recv()
     pl.semaphore_wait(all_here.at[1], NX - 1)
-    pl.semaphore_signal(all_here.at[2], inc=1, device_id=device(twin), device_id_type=BY_ID)
+    signal(all_here.at[2], twin)
     bound_all = jnp.concatenate([bound[i] for i in range(ANG)], axis=1)
-    for relay in relays:
-        relay.wait_recv()
+    half_m = m_full.at[pl.ds(0, spots)]
+    send(half_m, half_m, out_sem.at[4], relay_recv, twin).wait_recv()
     pl.semaphore_wait(all_here.at[2], 1)
 
     operator = m_full[...].reshape(PTS * ANG, PTS)
@@ -263,7 +292,7 @@
     weighted = [d[r * nb : (r + 1) * nb] * weight_ref[r] for r in range(shells)]
     wide = jnp.concatenate(weighted, axis=1).astype(BF16)
     terms = jnp.dot(wide, cont_t[...], preferred_element_type=F32)
-    for q in range(count // 128):
+    for q in range(count_c // 128):
         cut = turned(terms[:, q * 128 : (q + 1) * 128])
         for a in range(ANG):
             sendbuf[pl.ds(a * RAD + q * 8, 8)] = cut[a * 8 : a * 8 + 8]
@@ -275,19 +304,26 @@
         ).start()
 
     columns = [
-        device(((x + dx) % NX, (y + dy) % NY, 0, (core + dc) % NC)) for dx, dy, dc in PLANE
+        device((lax.rem(x + dx, NX), lax.rem(y + dy, NY), 0, lax.rem(core + dc, NC)))
+        for dx, dy, dc in PLANE
     ]
     for zs in (range(HALF), range(HALF, NZ)):
         for column in columns:
             for there in zs:
                 give(column + there * (NY * NC))
+    own_column = device((x, y, 0, core))
     for dz in (4, 3, 5, 2, 6, 1, 7):
-        give(device((x, y, (z + dz) % NZ, core)))
+        give(own_column + lax.rem(z + dz, NZ) * (NY * NC))
     pltpu.make_async_copy(
         sendbuf.at[pl.ds(me, 1)], recvbuf.at[pl.ds(me, 1)], end_recv
     ).start()
-    for copy in (rows, across, *along, *onward, *own, *relays):
-        copy.wait_send()
+    rows.wait_send()
+    across.wait_send()
+    for i in (2, 5):
+        send(three, three, out_sem.at[i], a_recv.at[1], twin).wait_send()
+    own_m = m_full.at[pl.ds(0, spots - 1)]
+    send(own_m, own_m, out_sem.at[3], relay_recv, twin).wait_send()
+    send(half_m, half_m, out_sem.at[4], relay_recv, twin).wait_send()
     pltpu.make_async_copy(sendbuf, recvbuf, end_recv).wait()
     row = jnp.sum(recvbuf[...], axis=0, keepdims=True)
     wide_row = jnp.broadcast_to(row, (8, 128))
@@ -306,7 +342,6 @@
     count = psi_cont.shape[1]
     any_space = pl.BlockSpec(memory_space=pl.ANY)
     dma = pltpu.SemaphoreType.DMA
-    n_peers = len(PEERS)
     return pl.pallas_call(
         kernel,
         out_shape=jax.ShapeDtypeStruct((nb // ANG, count // RAD), F32),
@@ -333,11 +368,11 @@
             pltpu.VMEM((ANG * RAD, 128), F32),
             pltpu.VMEM((ANG * RAD, 128), F32),
             dma((5,)),
-            dma((9 + 2 * n_peers,)),
-            dma((7,)),
+            dma((6,)),
+            dma((3,)),
             dma,
-            dma((n_peers,)),
-            dma((n_peers + 1,)),
+            dma((RAD // NC,)),
+            dma,
             dma,
             dma,
             pltpu.SemaphoreType.REGULAR((4,)),

time: 35.9 us -> 35.5 us (0.989)
  Pallas kernels: 34.5 us -> 34.1 us
    pallas_call x1, Pallas kernels: 34.5 us -> 34.1 us  [shards(): pl.pallas_call(kernel, out_shape=jax.ShapeDtypeStruct((nb // ANG, count /...]
where the time goes in v3:
time: 35.5 us; the launch traced here: 35.4 us
  Pallas kernels  34.1 us (96%)
  local copies, waits for them, and re-layouts  1.28 us (4%)
    pallas_call x1, Pallas kernels, shards(): pl.pallas_call(kernel, out_shape=jax.ShapeDtypeStruct((nb // ANG, count /...  34.1 us
    unnamed x1, local copies, waits for them, and re-layouts  1.28 us

profile of v3, /device:TPU:1, one launch (start us, length us, event | category | flops | bytes accessed | tf_op | source)
XLA Modules:
  0.0 35.4 jit_solution(5289157695818302745)
XLA Ops:
  0.0 34.1 %dipole.1 = f32[8,16]{1,0:T(8,128)} custom-call(bf16[128,128]{1,0:T(8,128)(2,1)} %bitcast.4, bf16[1024,128]{1,0:T(8,128)(2,1)} %bitcast.3, bf16[128,1024]{1,0:T(8,128)(2,1)} %ylm_hbm.1, f32[2]{0:T(128)} %weight_hbm.1, s32[8,128]{1,0:T(8,128)} %bitcast.5), custom_call_target="tpu_custom_call" | custom-call | tf_op jit(solution)/shard_map/dipole/pallas_call | solution.py:345
  34.1 1.3 %copy.7 = f32[8,16]{1,0:T(8,128)} copy(f32[8,16]{1,0:T(8,128)} %dipole.1) | data formatting | bytes 1024

commit v4 on v3

--- a/solution.py
+++ b/solution.py
@@ -29,11 +29,6 @@
 def device(place):
     x, y, z, core = place
     return x * (ANG * RAD // NX) + z * (NY * NC) + y * NC + core
-
-
-def turn_of(place):
-    x, y, z, core = place
-    return z * 32 + y * 8 + x * 2 + (1 - core)
 
 
 def piece_of(x, half, zl, y, core):
@@ -90,11 +85,10 @@
     first_spot = me - NC * spot
     edge = (zl == 0) | (zl == HALF - 1)
     z_other = jnp.where(edge, NZ - 1 - z, z)
-    turn = turn_of((x, y, z, core))
     to_x, from_x = lax.rem(x + y + 2, NX), lax.rem(x - y + 2 + NX, NX)
     rows_to, rows_from = (device((i, y, z_other, 1 - core)) for i in (to_x, from_x))
-    ahead_to, ahead_from = (turn < turn_of((i, y, z_other, 1 - core)) for i in (to_x, from_x))
-    count = lambda flag: jnp.where(flag, 1, 0)
+    y_peers = [me + (lax.rem(y + d, NY) - y) * NC for d in (2, 1, 3)]
+    zl_peers = [me + (lax.rem(zl + d, HALF) - zl) * NY * NC for d in (2, 1, 3)]
 
     def signal(semaphore, where):
         pl.semaphore_signal(semaphore, inc=1, device_id=where, device_id_type=BY_ID)
@@ -112,6 +106,10 @@
             device_id=where, device_id_type=BY_ID,
         )
 
+    barrier = pltpu.get_barrier_semaphore()
+    lines = (opposite, rows_from, rows_to, *zl_peers, *x_peers, *y_peers, twin)
+    for where in lines:
+        signal(barrier, where)
     loads = [
         pltpu.make_async_copy(ylm_hbm, ylm, local_sem.at[0]),
         pltpu.make_async_copy(order_hbm, order_ref, local_sem.at[3]),
@@ -122,37 +120,7 @@
     load_ylm, load_order, load_cont, load_bound, load_weight = loads
     for load in loads:
         load.start()
-
-    barrier = pltpu.get_barrier_semaphore()
-
-    @pl.when(ahead_from)
-    def _():
-        signal(barrier, rows_from)
-
-    @pl.when(ahead_to)
-    def _():
-        signal(barrier, rows_to)
-
-    @pl.when(half == 0)
-    def _():
-        signal(barrier, opposite)
-
-    each(x + 1, NX, lambda i: signal(barrier, me + (i - x) * x_step))
-
-    @pl.when(core == 1)
-    def _():
-        signal(barrier, twin)
-
-    each(spot + 1, RAD // NC, lambda i: signal(barrier, first_spot + NC * i))
-    before = 2 - count(ahead_from) - count(ahead_to) + half + x + (1 - core) + spot
-
-    @pl.when(before > 0)
-    def _():
-        pl.semaphore_wait(barrier, before)
-
-    @pl.when(jnp.logical_not(ahead_from))
-    def _():
-        signal(here.at[2], rows_from)
+    pl.semaphore_wait(barrier, len(lines))
 
     quarter_to = piece_of(to_x, lax.div(z_other, HALF), lax.rem(z_other, HALF), y, 1 - core)[1]
     rows = send(
@@ -161,37 +129,15 @@
     )
     across = send(bound_hbm, bound.at[ang], out_sem.at[1], a_recv.at[0], opposite)
 
-    @pl.when(jnp.logical_not(ahead_to))
-    def _():
-        rows.start()
-
-    each(0, x, lambda i: signal(here.at[0], me + (i - x) * x_step))
-
-    @pl.when(half == 1)
-    def _():
-        signal(here.at[1], opposite)
-        across.start()
-
-    @pl.when(core == 0)
-    def _():
-        signal(here.at[3], twin)
-
-    each(0, spot, lambda i: signal(here.at[3], first_spot + NC * i))
-
-    @pl.when(ahead_to)
-    def _():
-        pl.semaphore_wait(here.at[2], 1)
-        rows.start()
-
-    @pl.when(x < NX - 1)
-    def _():
-        pl.semaphore_wait(here.at[0], NX - 1 - x)
-
+    rows.start()
+    across.start()
     along = [
         send(bound_hbm, bound.at[ang], out_sem.at[2], a_recv.at[1], where) for where in x_peers
     ]
     for copy in along:
         copy.start()
+    for where in y_peers:
+        signal(here, where)
 
     load_order.wait()
     order = order_ref[...]
@@ -222,11 +168,6 @@
 
     lax.fori_loop(0, TOTAL // 128, couple, 0)
 
-    @pl.when(half == 0)
-    def _():
-        pl.semaphore_wait(here.at[1], 1)
-        across.start()
-
     def block_of(i):
         cls, quarter = piece_of(x, half, lax.div(i, NY), lax.rem(i, NY), core)
         return cls * (RAD // ANG) + quarter
@@ -235,11 +176,7 @@
     rows.wait_recv()
     mine[...] = jnp.dot(ys[...], z_ref[...], preferred_element_type=F32).astype(BF16)
     spots = RAD // NC
-    later_ones = spots - 1 - spot + core
-
-    @pl.when(later_ones > 0)
-    def _():
-        pl.semaphore_wait(here.at[3], later_ones)
+    pl.semaphore_wait(here, NY - 1)
 
     def give_piece(i):
         send(mine, m_full.at[block], out_sem.at[3], m_recv.at[spot], first_spot + NC * i).start()
@@ -375,7 +312,7 @@
             dma,
             dma,
             dma,
-            pltpu.SemaphoreType.REGULAR((4,)),
+            pltpu.SemaphoreType.REGULAR,
             pltpu.SemaphoreType.REGULAR((3,)),
         ],
         compiler_params=pltpu.CompilerParams(collective_id=0, has_side_effects=True),

time: 35.5 us -> 32.8 us (0.924)
  Pallas kernels: 34.1 us -> 31.4 us
    pallas_call x1, Pallas kernels: 34.1 us -> 31.4 us  [shards(): pl.pallas_call(kernel, out_shape=jax.ShapeDtypeStruct((nb // ANG, count /...]
where the time goes in v4:
time: 32.8 us; the launch traced here: 32.7 us
  Pallas kernels  31.4 us (96%)
  local copies, waits for them, and re-layouts  1.28 us (4%)
    pallas_call x1, Pallas kernels, shards(): pl.pallas_call(kernel, out_shape=jax.ShapeDtypeStruct((nb // ANG, count /...  31.4 us
    unnamed x1, local copies, waits for them, and re-layouts  1.28 us

profile of v4, /device:TPU:1, one launch (start us, length us, event | category | flops | bytes accessed | tf_op | source)
XLA Modules:
  0.0 32.7 jit_solution(17129968653973578289)
XLA Ops:
  0.0 31.4 %dipole.1 = f32[8,16]{1,0:T(8,128)} custom-call(bf16[128,128]{1,0:T(8,128)(2,1)} %bitcast.4, bf16[1024,128]{1,0:T(8,128)(2,1)} %bitcast.3, bf16[128,1024]{1,0:T(8,128)(2,1)} %ylm_hbm.1, f32[2]{0:T(128)} %weight_hbm.1, s32[8,128]{1,0:T(8,128)} %bitcast.5), custom_call_target="tpu_custom_call" | custom-call | tf_op jit(solution)/shard_map/dipole/pallas_call | solution.py:282
  31.4 1.3 %copy.7 = f32[8,16]{1,0:T(8,128)} copy(f32[8,16]{1,0:T(8,128)} %dipole.1) | data formatting | bytes 1024

commit v5 on v4

--- a/solution.py
+++ b/solution.py
@@ -70,9 +70,11 @@
 
 def kernel(
     bound_hbm, cont_hbm, ylm_hbm, weight_hbm, order_hbm, out_ref,
-    bound, cont, ylm, order_ref, weight_ref, ys, ncol, z_ref, mine, m_full, cont_t, sendbuf, recvbuf,
-    local_sem, out_sem, a_recv, f_recv, m_recv, relay_recv, end_send, end_recv, here, all_here,
+    bound, cont, ylm, order_ref, weight_ref, ys, ncol, z_ref, mine, m_full, cont_t, *rest
 ):
+    sendbufs, (recvbuf, *semaphores) = rest[:HALF], rest[HALF:]
+    local_sem, out_sem, a_recv, f_recv, m_recv, relay_recv, end_send, end_recv, *signals = semaphores
+    here, answer, all_here = signals
     ang, rad = lax.axis_index("ang"), lax.axis_index("rad")
     x, half, core, spot = lax.div(ang, 2), lax.rem(ang, 2), lax.rem(rad, NC), lax.div(rad, NC)
     zl, y = lax.div(spot, NY), lax.rem(spot, NY)
@@ -107,9 +109,14 @@
         )
 
     barrier = pltpu.get_barrier_semaphore()
-    lines = (opposite, rows_from, rows_to, *zl_peers, *x_peers, *y_peers, twin)
+    lines = (rows_from, rows_to, *zl_peers, *x_peers, *y_peers, twin)
     for where in lines:
         signal(barrier, where)
+
+    @pl.when(half == 0)
+    def _():
+        signal(barrier, opposite)
+
     loads = [
         pltpu.make_async_copy(ylm_hbm, ylm, local_sem.at[0]),
         pltpu.make_async_copy(order_hbm, order_ref, local_sem.at[3]),
@@ -120,17 +127,21 @@
     load_ylm, load_order, load_cont, load_bound, load_weight = loads
     for load in loads:
         load.start()
-    pl.semaphore_wait(barrier, len(lines))
+    pl.semaphore_wait(barrier, len(lines) + half)
 
     quarter_to = piece_of(to_x, lax.div(z_other, HALF), lax.rem(z_other, HALF), y, 1 - core)[1]
     rows = send(
         ylm_hbm.at[pl.ds(pl.multiple_of(quarter_to * PIECE, PIECE), PIECE)],
         ys, out_sem.at[0], f_recv, rows_to,
     )
-    across = send(bound_hbm, bound.at[ang], out_sem.at[1], a_recv.at[0], opposite)
-
     rows.start()
-    across.start()
+    mine_across = send(bound_hbm, bound.at[ang], out_sem.at[1], a_recv.at[0], opposite)
+
+    @pl.when(half == 1)
+    def _():
+        signal(answer, opposite)
+        mine_across.start()
+
     along = [
         send(bound_hbm, bound.at[ang], out_sem.at[2], a_recv.at[1], where) for where in x_peers
     ]
@@ -167,6 +178,17 @@
         return carry
 
     lax.fori_loop(0, TOTAL // 128, couple, 0)
+    three = bound.at[pl.ds(0, NX - 1)]
+    send(three, three, out_sem.at[2], a_recv.at[1], twin).wait_recv()
+
+    @pl.when(half == 0)
+    def _():
+        pl.semaphore_wait(answer, 1)
+        mine_across.start()
+        for d in range(1, NX):
+            there = bound.at[2 * lax.rem(x + d, NX)]
+            send(there, there, out_sem.at[1], a_recv.at[0], opposite).start()
+
 
     def block_of(i):
         cls, quarter = piece_of(x, half, lax.div(i, NY), lax.rem(i, NY), core)
@@ -178,20 +200,26 @@
     spots = RAD // NC
     pl.semaphore_wait(here, NY - 1)
 
-    def give_piece(i):
-        send(mine, m_full.at[block], out_sem.at[3], m_recv.at[spot], first_spot + NC * i).start()
-
-    each(spot + 1, spots, give_piece)
-    each(0, spot, give_piece)
+    far, step = jnp.where(zl < HALF // 2, HALF - 1, 0), jnp.where(zl < HALF // 2, -1, 1)
+    there = [
+        ang * RAD + (far + step * k) * NY * NC + lax.rem(y + d, NY) * NC + core
+        for k in range(HALF)
+        for d in (2, 1, 3)
+    ]
+    for where in (*there[:6], *zl_peers, *there[6:]):
+        send(mine, m_full.at[block], out_sem.at[3], m_recv.at[spot], where).start()
     send(mine, m_full.at[block], out_sem.at[4], relay_recv, twin).start()
     m_full[block] = mine[...]
 
     signal(all_here.at[0], opposite)
-    across.wait_recv()
-    other_cls = bound.at[ang + 1 - 2 * half]
-    onward = [send(other_cls, other_cls, out_sem.at[5], a_recv.at[2], where) for where in x_peers]
-    for copy in onward:
-        copy.start()
+
+    @pl.when(half == 0)
+    def _():
+        mine_across.wait_recv()
+        other = bound.at[ang + 1]
+        for where in x_peers:
+            send(other, other, out_sem.at[5], a_recv.at[2], where).start()
+
     pl.semaphore_wait(all_here.at[0], 1)
     for where in x_peers:
         signal(all_here.at[1], where)
@@ -213,9 +241,17 @@
     each(spot + 1, spots, pass_on)
     load_bound.wait()
     load_weight.wait()
-    three = bound.at[pl.ds(0, NX - 1)]
-    for i in (1, 2):
-        send(three, three, out_sem.at[2], a_recv.at[i], twin).wait_recv()
+
+    @pl.when(half == 0)
+    def _():
+        send(three, three, out_sem.at[5], a_recv.at[2], twin).wait()
+
+    four = bound.at[pl.ds(0, NX)]
+
+    @pl.when(half == 1)
+    def _():
+        send(four, four, out_sem.at[1], a_recv.at[0], twin).wait_recv()
+
     pl.semaphore_wait(all_here.at[1], NX - 1)
     signal(all_here.at[2], twin)
     bound_all = jnp.concatenate([bound[i] for i in range(ANG)], axis=1)
@@ -228,40 +264,57 @@
     nb = d.shape[0] // shells
     weighted = [d[r * nb : (r + 1) * nb] * weight_ref[r] for r in range(shells)]
     wide = jnp.concatenate(weighted, axis=1).astype(BF16)
-    terms = jnp.dot(wide, cont_t[...], preferred_element_type=F32)
-    for q in range(count_c // 128):
-        cut = turned(terms[:, q * 128 : (q + 1) * 128])
-        for a in range(ANG):
-            sendbuf[pl.ds(a * RAD + q * 8, 8)] = cut[a * 8 : a * 8 + 8]
-
-    def give(number):
+
+    def give(q, row, number):
         pltpu.make_async_remote_copy(
-            src_ref=sendbuf.at[pl.ds(number, 1)], dst_ref=recvbuf.at[pl.ds(me, 1)],
+            src_ref=sendbufs[q].at[pl.ds(row, 1)], dst_ref=recvbuf.at[pl.ds(me, 1)],
             send_sem=end_send, recv_sem=end_recv, device_id=number, device_id_type=BY_ID,
         ).start()
 
-    columns = [
-        device((lax.rem(x + dx, NX), lax.rem(y + dy, NY), 0, lax.rem(core + dc, NC)))
-        for dx, dy, dc in PLANE
-    ]
-    for zs in (range(HALF), range(HALF, NZ)):
-        for column in columns:
-            for there in zs:
-                give(column + there * (NY * NC))
-    own_column = device((x, y, 0, core))
-    for dz in (4, 3, 5, 2, 6, 1, 7):
-        give(own_column + lax.rem(z + dz, NZ) * (NY * NC))
-    pltpu.make_async_copy(
-        sendbuf.at[pl.ds(me, 1)], recvbuf.at[pl.ds(me, 1)], end_recv
-    ).start()
+    columns = []
+    for dx, dy, dc in PLANE:
+        there_x = lax.rem(x + dx, NX)
+        there_yc = lax.rem(y + dy, NY) * NC + lax.rem(core + dc, NC)
+        columns.append((there_x * 16 + there_yc, there_x * x_step + there_yc))
+    for q in range(HALF):
+        terms = jnp.dot(
+            wide, cont_t[:, pl.ds(q * 128, 128)], preferred_element_type=F32
+        )
+        sendbufs[q][...] = turned(terms)
+        for row, number in columns:
+            give(q, row, number + q * NY * NC)
+    for q in range(HALF):
+        for row, number in columns:
+            give(q, row + 8, number + (q + HALF) * NY * NC)
+    own_yc = y * NC + core
+    for there in range(NZ):
+        q, row = there % HALF, x * 16 + there // HALF * 8 + own_yc
+
+        @pl.when(z != there)
+        def _():
+            give(q, row, x * x_step + there * NY * NC + own_yc)
+
+        @pl.when(z == there)
+        def _():
+            pltpu.make_async_copy(
+                sendbufs[q].at[pl.ds(row, 1)], recvbuf.at[pl.ds(me, 1)], end_recv
+            ).start()
+
     rows.wait_send()
-    across.wait_send()
-    for i in (2, 5):
-        send(three, three, out_sem.at[i], a_recv.at[1], twin).wait_send()
+
+    @pl.when(half == 0)
+    def _():
+        send(four, four, out_sem.at[1], a_recv.at[0], twin).wait_send()
+
+    @pl.when(half == 1)
+    def _():
+        mine_across.wait_send()
+
+    send(three, three, out_sem.at[2], a_recv.at[1], twin).wait_send()
     own_m = m_full.at[pl.ds(0, spots - 1)]
     send(own_m, own_m, out_sem.at[3], relay_recv, twin).wait_send()
     send(half_m, half_m, out_sem.at[4], relay_recv, twin).wait_send()
-    pltpu.make_async_copy(sendbuf, recvbuf, end_recv).wait()
+    pltpu.make_async_copy(recvbuf, recvbuf, end_recv).wait()
     row = jnp.sum(recvbuf[...], axis=0, keepdims=True)
     wide_row = jnp.broadcast_to(row, (8, 128))
     at = lax.broadcasted_iota(jnp.int32, (8, 128), 0)
@@ -269,9 +322,8 @@
     for j in range(1, 8):
         spread = jnp.where(at == j, pltpu.roll(wide_row, 128 - 16 * j, 1), spread)
     out_ref[...] = spread[:, : out_ref.shape[1]]
-    pltpu.make_async_copy(
-        sendbuf.at[pl.ds(0, ANG * RAD - 1)], recvbuf.at[pl.ds(0, ANG * RAD - 1)], end_send
-    ).wait()
+    sent = recvbuf.at[pl.ds(0, ANG * RAD - 1)]
+    pltpu.make_async_copy(sent, sent, end_send).wait()
 
 
 def shards(psi_bound, psi_cont, ylm, radial_weight, order):
@@ -302,7 +354,7 @@
             pltpu.VMEM((PIECE, points), BF16),
             pltpu.VMEM((RAD, PIECE, points), BF16),
             pltpu.VMEM((shells * points, count), BF16),
-            pltpu.VMEM((ANG * RAD, 128), F32),
+            *[pltpu.VMEM((64, 128), F32)] * HALF,
             pltpu.VMEM((ANG * RAD, 128), F32),
             dma((5,)),
             dma((6,)),
@@ -312,6 +364,7 @@
             dma,
             dma,
             dma,
+            pltpu.SemaphoreType.REGULAR,
             pltpu.SemaphoreType.REGULAR,
             pltpu.SemaphoreType.REGULAR((3,)),
         ],

time: 32.8 us -> 32.8 us (level)
  no operation moved by 1% of the time
where the time goes in v5:
time: 32.8 us; the launch traced here: 32.7 us
  Pallas kernels  31.4 us (96%)
  local copies, waits for them, and re-layouts  1.28 us (4%)
    pallas_call x1, Pallas kernels, shards(): pl.pallas_call(kernel, out_shape=jax.ShapeDtypeStruct((nb // ANG, count /...  31.4 us
    unnamed x1, local copies, waits for them, and re-layouts  1.28 us

profile of v5, /device:TPU:1, one launch (start us, length us, event | category | flops | bytes accessed | tf_op | source)
XLA Modules:
  0.0 32.7 jit_solution(5447018443699137081)
XLA Ops:
  0.0 31.4 %dipole.1 = f32[8,16]{1,0:T(8,128)} custom-call(bf16[128,128]{1,0:T(8,128)(2,1)} %bitcast.4, bf16[1024,128]{1,0:T(8,128)(2,1)} %bitcast.3, bf16[128,1024]{1,0:T(8,128)(2,1)} %ylm_hbm.1, f32[2]{0:T(128)} %weight_hbm.1, s32[8,128]{1,0:T(8,128)} %bitcast.5), custom_call_target="tpu_custom_call" | custom-call | tf_op jit(solution)/shard_map/dipole/pallas_call | solution.py:334
  31.4 1.3 %copy.7 = f32[8,16]{1,0:T(8,128)} copy(f32[8,16]{1,0:T(8,128)} %dipole.1) | data formatting | bytes 1024

commit v6 on v5

--- a/solution.py
+++ b/solution.py
@@ -23,6 +23,7 @@
     ((dx, dy, dc) for dx in range(NX) for dy in range(NY) for dc in range(NC) if (dx, dy, dc) != (0, 0, 0)),
     key=lambda o: -(ring(o[0], NX) + ring(o[1], NY)),
 )
+FAR = 4
 BY_ID = pl.DeviceIdType.LOGICAL
 
 
@@ -74,7 +75,7 @@
 ):
     sendbufs, (recvbuf, *semaphores) = rest[:HALF], rest[HALF:]
     local_sem, out_sem, a_recv, f_recv, m_recv, relay_recv, end_send, end_recv, *signals = semaphores
-    here, answer, all_here = signals
+    here, both, answer, all_here = signals
     ang, rad = lax.axis_index("ang"), lax.axis_index("rad")
     x, half, core, spot = lax.div(ang, 2), lax.rem(ang, 2), lax.rem(rad, NC), lax.div(rad, NC)
     zl, y = lax.div(spot, NY), lax.rem(spot, NY)
@@ -135,18 +136,11 @@
         ys, out_sem.at[0], f_recv, rows_to,
     )
     rows.start()
-    mine_across = send(bound_hbm, bound.at[ang], out_sem.at[1], a_recv.at[0], opposite)
 
     @pl.when(half == 1)
     def _():
         signal(answer, opposite)
-        mine_across.start()
-
-    along = [
-        send(bound_hbm, bound.at[ang], out_sem.at[2], a_recv.at[1], where) for where in x_peers
-    ]
-    for copy in along:
-        copy.start()
+
     for where in y_peers:
         signal(here, where)
 
@@ -178,17 +172,17 @@
         return carry
 
     lax.fori_loop(0, TOTAL // 128, couple, 0)
-    three = bound.at[pl.ds(0, NX - 1)]
-    send(three, three, out_sem.at[2], a_recv.at[1], twin).wait_recv()
+    for where in x_peers:
+        send(bound_hbm, bound.at[ang], out_sem.at[2], a_recv.at[1], where).start()
+    across = send(bound_hbm, bound.at[ang], out_sem.at[1], a_recv.at[0], opposite)
 
     @pl.when(half == 0)
     def _():
         pl.semaphore_wait(answer, 1)
-        mine_across.start()
-        for d in range(1, NX):
-            there = bound.at[2 * lax.rem(x + d, NX)]
-            send(there, there, out_sem.at[1], a_recv.at[0], opposite).start()
-
+
+    across.start()
+    pl.semaphore_wait(here, NY - 1)
+    signal(both, twin)
 
     def block_of(i):
         cls, quarter = piece_of(x, half, lax.div(i, NY), lax.rem(i, NY), core)
@@ -198,28 +192,37 @@
     rows.wait_recv()
     mine[...] = jnp.dot(ys[...], z_ref[...], preferred_element_type=F32).astype(BF16)
     spots = RAD // NC
-    pl.semaphore_wait(here, NY - 1)
+    pl.semaphore_wait(both, 1)
 
     far, step = jnp.where(zl < HALF // 2, HALF - 1, 0), jnp.where(zl < HALF // 2, -1, 1)
-    there = [
-        ang * RAD + (far + step * k) * NY * NC + lax.rem(y + d, NY) * NC + core
-        for k in range(HALF)
-        for d in (2, 1, 3)
-    ]
-    for where in (*there[:6], *zl_peers, *there[6:]):
+    flip = 1 - 2 * core
+    there = [(far + step * k, d) for k in range(HALF) for d in (2, 1, 3)]
+
+    def give_piece(where):
         send(mine, m_full.at[block], out_sem.at[3], m_recv.at[spot], where).start()
+
+    def give_far_piece(zl_there, d):
+        where = ang * RAD + zl_there * NY * NC + lax.rem(y + d, NY) * NC + core
+        give_piece(where)
+
+        @pl.when(jnp.abs(zl_there - zl) + ring(d, NY) >= FAR)
+        def _():
+            send(mine, m_full.at[block], out_sem.at[4], relay_recv, where + flip).start()
+
+    for zl_there, d in there[:6]:
+        give_far_piece(zl_there, d)
+    for where in zl_peers:
+        give_piece(where)
+    for zl_there, d in there[6:]:
+        give_far_piece(zl_there, d)
     send(mine, m_full.at[block], out_sem.at[4], relay_recv, twin).start()
     m_full[block] = mine[...]
 
     signal(all_here.at[0], opposite)
-
-    @pl.when(half == 0)
-    def _():
-        mine_across.wait_recv()
-        other = bound.at[ang + 1]
-        for where in x_peers:
-            send(other, other, out_sem.at[5], a_recv.at[2], where).start()
-
+    across.wait_recv()
+    other = bound.at[ang + 1 - 2 * half]
+    for where in x_peers:
+        send(other, other, out_sem.at[5], a_recv.at[2], where).start()
     pl.semaphore_wait(all_here.at[0], 1)
     for where in x_peers:
         signal(all_here.at[1], where)
@@ -235,23 +238,19 @@
     def pass_on(i):
         there = m_full.at[block_of(i)]
         send(there, there, out_sem.at[4], m_recv.at[i], twin).wait_recv()
-        send(there, there, out_sem.at[4], relay_recv, twin).start()
+        dy = jnp.abs(lax.rem(i, NY) - y)
+
+        @pl.when(jnp.abs(lax.div(i, NY) - zl) + jnp.minimum(dy, NY - dy) < FAR)
+        def _():
+            send(there, there, out_sem.at[4], relay_recv, twin).start()
 
     each(0, spot, pass_on)
     each(spot + 1, spots, pass_on)
     load_bound.wait()
     load_weight.wait()
-
-    @pl.when(half == 0)
-    def _():
-        send(three, three, out_sem.at[5], a_recv.at[2], twin).wait()
-
-    four = bound.at[pl.ds(0, NX)]
-
-    @pl.when(half == 1)
-    def _():
-        send(four, four, out_sem.at[1], a_recv.at[0], twin).wait_recv()
-
+    three = bound.at[pl.ds(0, NX - 1)]
+    for i in (1, 2):
+        send(three, three, out_sem.at[2], a_recv.at[i], twin).wait_recv()
     pl.semaphore_wait(all_here.at[1], NX - 1)
     signal(all_here.at[2], twin)
     bound_all = jnp.concatenate([bound[i] for i in range(ANG)], axis=1)
@@ -301,16 +300,9 @@
             ).start()
 
     rows.wait_send()
-
-    @pl.when(half == 0)
-    def _():
-        send(four, four, out_sem.at[1], a_recv.at[0], twin).wait_send()
-
-    @pl.when(half == 1)
-    def _():
-        mine_across.wait_send()
-
-    send(three, three, out_sem.at[2], a_recv.at[1], twin).wait_send()
+    across.wait_send()
+    for i in (2, 5):
+        send(three, three, out_sem.at[i], a_recv.at[1], twin).wait_send()
     own_m = m_full.at[pl.ds(0, spots - 1)]
     send(own_m, own_m, out_sem.at[3], relay_recv, twin).wait_send()
     send(half_m, half_m, out_sem.at[4], relay_recv, twin).wait_send()
@@ -364,8 +356,7 @@
             dma,
             dma,
             dma,
-            pltpu.SemaphoreType.REGULAR,
-            pltpu.SemaphoreType.REGULAR,
+            *[pltpu.SemaphoreType.REGULAR] * 3,
             pltpu.SemaphoreType.REGULAR((3,)),
         ],
         compiler_params=pltpu.CompilerParams(collective_id=0, has_side_effects=True),

time: 32.8 us -> 33.2 us (1.012)
  Pallas kernels: 31.4 us -> 31.8 us
    pallas_call x1, Pallas kernels: 31.4 us -> 31.8 us  [shards(): pl.pallas_call(kernel, out_shape=jax.ShapeDtypeStruct((nb // ANG, count /...]
where the time goes in v6:
time: 33.2 us; the launch traced here: 33.1 us
  Pallas kernels  31.8 us (96%)
  local copies, waits for them, and re-layouts  1.28 us (4%)
    pallas_call x1, Pallas kernels, shards(): pl.pallas_call(kernel, out_shape=jax.ShapeDtypeStruct((nb // ANG, count /...  31.8 us
    unnamed x1, local copies, waits for them, and re-layouts  1.28 us

profile of v6, /device:TPU:1, one launch (start us, length us, event | category | flops | bytes accessed | tf_op | source)
XLA Modules:
  0.0 33.1 jit_solution(17400205340395951803)
XLA Ops:
  0.0 31.8 %dipole.1 = f32[8,16]{1,0:T(8,128)} custom-call(bf16[128,128]{1,0:T(8,128)(2,1)} %bitcast.4, bf16[1024,128]{1,0:T(8,128)(2,1)} %bitcast.3, bf16[128,1024]{1,0:T(8,128)(2,1)} %ylm_hbm.1, f32[2]{0:T(128)} %weight_hbm.1, s32[8,128]{1,0:T(8,128)} %bitcast.5), custom_call_target="tpu_custom_call" | custom-call | tf_op jit(solution)/shard_map/dipole/pallas_call | solution.py:326
  31.8 1.3 %copy.7 = f32[8,16]{1,0:T(8,128)} copy(f32[8,16]{1,0:T(8,128)} %dipole.1) | data formatting | bytes 1024

commit v7 on v6

--- a/solution.py
+++ b/solution.py
@@ -23,7 +23,7 @@
     ((dx, dy, dc) for dx in range(NX) for dy in range(NY) for dc in range(NC) if (dx, dy, dc) != (0, 0, 0)),
     key=lambda o: -(ring(o[0], NX) + ring(o[1], NY)),
 )
-FAR = 4
+NEXT = 2
 BY_ID = pl.DeviceIdType.LOGICAL
 
 
@@ -132,9 +132,10 @@
 
     quarter_to = piece_of(to_x, lax.div(z_other, HALF), lax.rem(z_other, HALF), y, 1 - core)[1]
     rows = send(
-        ylm_hbm.at[pl.ds(pl.multiple_of(quarter_to * PIECE, PIECE), PIECE)],
+        ylm.at[pl.ds(pl.multiple_of(quarter_to * PIECE, PIECE), PIECE)],
         ys, out_sem.at[0], f_recv, rows_to,
     )
+    load_ylm.wait()
     rows.start()
 
     @pl.when(half == 1)
@@ -150,7 +151,6 @@
     orderf = order.astype(F32)
     for s in range(TOTAL // 128):
         ncol[pl.ds(s * 128, 128)] = jnp.broadcast_to(orderf[s : s + 1], (128, 128)).T
-    load_ylm.wait()
 
     def couple(s, carry):
         here = pl.ds(pl.multiple_of(s * 128, 128), 128)
@@ -181,6 +181,14 @@
         pl.semaphore_wait(answer, 1)
 
     across.start()
+    load_cont.wait()
+    shells = weight_ref.shape[0]
+    count_c = cont.shape[0] // shells
+    for r in range(shells):
+        for c in range(count_c // 128):
+            part = cont[pl.ds(r * count_c + c * 128, 128)].astype(F32).T
+            cont_t[pl.ds(r * 128, 128), pl.ds(c * 128, 128)] = part.astype(BF16)
+
     pl.semaphore_wait(here, NY - 1)
     signal(both, twin)
 
@@ -195,26 +203,26 @@
     pl.semaphore_wait(both, 1)
 
     far, step = jnp.where(zl < HALF // 2, HALF - 1, 0), jnp.where(zl < HALF // 2, -1, 1)
-    flip = 1 - 2 * core
-    there = [(far + step * k, d) for k in range(HALF) for d in (2, 1, 3)]
-
-    def give_piece(where):
-        send(mine, m_full.at[block], out_sem.at[3], m_recv.at[spot], where).start()
-
-    def give_far_piece(zl_there, d):
-        where = ang * RAD + zl_there * NY * NC + lax.rem(y + d, NY) * NC + core
-        give_piece(where)
-
-        @pl.when(jnp.abs(zl_there - zl) + ring(d, NY) >= FAR)
-        def _():
-            send(mine, m_full.at[block], out_sem.at[4], relay_recv, where + flip).start()
-
-    for zl_there, d in there[:6]:
-        give_far_piece(zl_there, d)
-    for where in zl_peers:
-        give_piece(where)
-    for zl_there, d in there[6:]:
-        give_far_piece(zl_there, d)
+
+    def give_pieces(own_k, both_from):
+        for k in range(HALF):
+            for d in (2, 1, 3, 0):
+                if (k, d) == (own_k, 0):
+                    continue
+                where = ang * RAD + (far + step * k) * NY * NC + lax.rem(y + d, NY) * NC + core
+                send(mine, m_full.at[block], out_sem.at[3], m_recv.at[spot], where).start()
+                if both_from and own_k - k + ring(d, NY) >= both_from:
+                    where = where + 1 - 2 * core
+                    send(mine, m_full.at[block], out_sem.at[6], relay_recv, where).start()
+
+    @pl.when(edge)
+    def _():
+        give_pieces(HALF - 1, NEXT)
+
+    @pl.when(jnp.logical_not(edge))
+    def _():
+        give_pieces(HALF // 2, 0)
+
     send(mine, m_full.at[block], out_sem.at[4], relay_recv, twin).start()
     m_full[block] = mine[...]
 
@@ -227,25 +235,23 @@
     for where in x_peers:
         signal(all_here.at[1], where)
 
-    load_cont.wait()
-    shells = weight_ref.shape[0]
-    count_c = cont.shape[0] // shells
-    for r in range(shells):
-        for c in range(count_c // 128):
-            part = cont[pl.ds(r * count_c + c * 128, 128)].astype(F32).T
-            cont_t[pl.ds(r * 128, 128), pl.ds(c * 128, 128)] = part.astype(BF16)
-
-    def pass_on(i):
-        there = m_full.at[block_of(i)]
-        send(there, there, out_sem.at[4], m_recv.at[i], twin).wait_recv()
-        dy = jnp.abs(lax.rem(i, NY) - y)
-
-        @pl.when(jnp.abs(lax.div(i, NY) - zl) + jnp.minimum(dy, NY - dy) < FAR)
-        def _():
-            send(there, there, out_sem.at[4], relay_recv, twin).start()
-
-    each(0, spot, pass_on)
-    each(spot + 1, spots, pass_on)
+    def pass_on(start, end, limit):
+        def act(i):
+            @pl.when(i != spot)
+            def _():
+                there = m_full.at[block_of(i)]
+                send(there, there, out_sem.at[4], m_recv.at[i], twin).wait_recv()
+                dy = jnp.abs(lax.rem(i, NY) - y)
+
+                @pl.when(jnp.abs(lax.div(i, NY) - zl) + jnp.minimum(dy, NY - dy) < limit)
+                def _():
+                    send(there, there, out_sem.at[4], relay_recv, twin).start()
+
+        each(start, end, act)
+
+    pass_on(NY, spots - NY, spots)
+    pass_on(0, NY, NEXT)
+    pass_on(spots - NY, spots, NEXT)
     load_bound.wait()
     load_weight.wait()
     three = bound.at[pl.ds(0, NX - 1)]
@@ -305,7 +311,20 @@
         send(three, three, out_sem.at[i], a_recv.at[1], twin).wait_send()
     own_m = m_full.at[pl.ds(0, spots - 1)]
     send(own_m, own_m, out_sem.at[3], relay_recv, twin).wait_send()
-    send(half_m, half_m, out_sem.at[4], relay_recv, twin).wait_send()
+
+    def sent_pieces(i, n):
+        part = m_full.at[pl.ds(0, n)]
+        send(part, part, out_sem.at[i], relay_recv, twin).wait_send()
+
+    @pl.when(edge)
+    def _():
+        sent_pieces(4, 11)
+        sent_pieces(6, 12)
+
+    @pl.when(jnp.logical_not(edge))
+    def _():
+        sent_pieces(4, 9)
+
     pltpu.make_async_copy(recvbuf, recvbuf, end_recv).wait()
     row = jnp.sum(recvbuf[...], axis=0, keepdims=True)
     wide_row = jnp.broadcast_to(row, (8, 128))
@@ -349,7 +368,7 @@
             *[pltpu.VMEM((64, 128), F32)] * HALF,
             pltpu.VMEM((ANG * RAD, 128), F32),
             dma((5,)),
-            dma((6,)),
+            dma((7,)),
             dma((3,)),
             dma,
             dma((RAD // NC,)),

time: 33.2 us -> 32.5 us (0.979)
  Pallas kernels: 31.8 us -> 31.1 us
    pallas_call x1, Pallas kernels: 31.8 us -> 31.1 us  [shards(): pl.pallas_call(kernel, out_shape=jax.ShapeDtypeStruct((nb // ANG, count /...]
where the time goes in v7:
time: 32.5 us; the launch traced here: 32.4 us
  Pallas kernels  31.1 us (96%)
  local copies, waits for them, and re-layouts  1.28 us (4%)
    pallas_call x1, Pallas kernels, shards(): pl.pallas_call(kernel, out_shape=jax.ShapeDtypeStruct((nb // ANG, count /...  31.1 us
    unnamed x1, local copies, waits for them, and re-layouts  1.28 us

profile of v7, /device:TPU:1, one launch (start us, length us, event | category | flops | bytes accessed | tf_op | source)
XLA Modules:
  0.0 32.4 jit_solution(1347504808089070044)
XLA Ops:
  0.0 31.1 %dipole.1 = f32[8,16]{1,0:T(8,128)} custom-call(bf16[128,128]{1,0:T(8,128)(2,1)} %bitcast.4, bf16[1024,128]{1,0:T(8,128)(2,1)} %bitcast.3, bf16[128,1024]{1,0:T(8,128)(2,1)} %ylm_hbm.1, f32[2]{0:T(128)} %weight_hbm.1, s32[8,128]{1,0:T(8,128)} %bitcast.5), custom_call_target="tpu_custom_call" | custom-call | tf_op jit(solution)/shard_map/dipole/pallas_call | solution.py:345
  31.2 1.3 %copy.7 = f32[8,16]{1,0:T(8,128)} copy(f32[8,16]{1,0:T(8,128)} %dipole.1) | data formatting | bytes 1024

commit v8 on v7

--- a/solution.py
+++ b/solution.py
@@ -75,7 +75,7 @@
 ):
     sendbufs, (recvbuf, *semaphores) = rest[:HALF], rest[HALF:]
     local_sem, out_sem, a_recv, f_recv, m_recv, relay_recv, end_send, end_recv, *signals = semaphores
-    here, both, answer, all_here = signals
+    here, both, all_here = signals
     ang, rad = lax.axis_index("ang"), lax.axis_index("rad")
     x, half, core, spot = lax.div(ang, 2), lax.rem(ang, 2), lax.rem(rad, NC), lax.div(rad, NC)
     zl, y = lax.div(spot, NY), lax.rem(spot, NY)
@@ -110,14 +110,9 @@
         )
 
     barrier = pltpu.get_barrier_semaphore()
-    lines = (rows_from, rows_to, *zl_peers, *x_peers, *y_peers, twin)
+    lines = (rows_from, opposite, rows_to, *zl_peers, *x_peers, *y_peers, twin)
     for where in lines:
         signal(barrier, where)
-
-    @pl.when(half == 0)
-    def _():
-        signal(barrier, opposite)
-
     loads = [
         pltpu.make_async_copy(ylm_hbm, ylm, local_sem.at[0]),
         pltpu.make_async_copy(order_hbm, order_ref, local_sem.at[3]),
@@ -128,7 +123,7 @@
     load_ylm, load_order, load_cont, load_bound, load_weight = loads
     for load in loads:
         load.start()
-    pl.semaphore_wait(barrier, len(lines) + half)
+    pl.semaphore_wait(barrier, len(lines))
 
     quarter_to = piece_of(to_x, lax.div(z_other, HALF), lax.rem(z_other, HALF), y, 1 - core)[1]
     rows = send(
@@ -138,9 +133,11 @@
     load_ylm.wait()
     rows.start()
 
-    @pl.when(half == 1)
-    def _():
-        signal(answer, opposite)
+    across = send(bound_hbm, bound.at[ang], out_sem.at[1], a_recv.at[0], opposite)
+
+    @pl.when(half == 0)
+    def _():
+        across.start()
 
     for where in y_peers:
         signal(here, where)
@@ -174,13 +171,11 @@
     lax.fori_loop(0, TOTAL // 128, couple, 0)
     for where in x_peers:
         send(bound_hbm, bound.at[ang], out_sem.at[2], a_recv.at[1], where).start()
-    across = send(bound_hbm, bound.at[ang], out_sem.at[1], a_recv.at[0], opposite)
-
-    @pl.when(half == 0)
-    def _():
-        pl.semaphore_wait(answer, 1)
-
-    across.start()
+
+    @pl.when(half == 1)
+    def _():
+        across.start()
+
     load_cont.wait()
     shells = weight_ref.shape[0]
     count_c = cont.shape[0] // shells
@@ -211,7 +206,7 @@
                     continue
                 where = ang * RAD + (far + step * k) * NY * NC + lax.rem(y + d, NY) * NC + core
                 send(mine, m_full.at[block], out_sem.at[3], m_recv.at[spot], where).start()
-                if both_from and own_k - k + ring(d, NY) >= both_from:
+                if both_from and own_k - k >= both_from:
                     where = where + 1 - 2 * core
                     send(mine, m_full.at[block], out_sem.at[6], relay_recv, where).start()
 
@@ -241,9 +236,8 @@
             def _():
                 there = m_full.at[block_of(i)]
                 send(there, there, out_sem.at[4], m_recv.at[i], twin).wait_recv()
-                dy = jnp.abs(lax.rem(i, NY) - y)
-
-                @pl.when(jnp.abs(lax.div(i, NY) - zl) + jnp.minimum(dy, NY - dy) < limit)
+
+                @pl.when(jnp.abs(lax.div(i, NY) - zl) < limit)
                 def _():
                     send(there, there, out_sem.at[4], relay_recv, twin).start()
 
@@ -316,14 +310,11 @@
         part = m_full.at[pl.ds(0, n)]
         send(part, part, out_sem.at[i], relay_recv, twin).wait_send()
 
+    sent_pieces(4, spots - NY)
+
     @pl.when(edge)
     def _():
-        sent_pieces(4, 11)
-        sent_pieces(6, 12)
-
-    @pl.when(jnp.logical_not(edge))
-    def _():
-        sent_pieces(4, 9)
+        sent_pieces(6, 2 * NY)
 
     pltpu.make_async_copy(recvbuf, recvbuf, end_recv).wait()
     row = jnp.sum(recvbuf[...], axis=0, keepdims=True)
@@ -375,7 +366,7 @@
             dma,
             dma,
             dma,
-            *[pltpu.SemaphoreType.REGULAR] * 3,
+            *[pltpu.SemaphoreType.REGULAR] * 2,
             pltpu.SemaphoreType.REGULAR((3,)),
         ],
         compiler_params=pltpu.CompilerParams(collective_id=0, has_side_effects=True),

time: 32.5 us -> 32.2 us (level)
    pallas_call x1, Pallas kernels: 31.1 us -> 30.8 us  [shards(): pl.pallas_call(kernel, out_shape=jax.ShapeDtypeStruct((nb // ANG, count /...]
where the time goes in v8:
time: 32.2 us; the launch traced here: 32.1 us
  Pallas kernels  30.8 us (96%)
  local copies, waits for them, and re-layouts  1.28 us (4%)
    pallas_call x1, Pallas kernels, shards(): pl.pallas_call(kernel, out_shape=jax.ShapeDtypeStruct((nb // ANG, count /...  30.8 us
    unnamed x1, local copies, waits for them, and re-layouts  1.28 us

profile of v8, /device:TPU:1, one launch (start us, length us, event | category | flops | bytes accessed | tf_op | source)
XLA Modules:
  0.0 32.1 jit_solution(9842708771395689354)
XLA Ops:
  0.0 30.8 %dipole.1 = f32[8,16]{1,0:T(8,128)} custom-call(bf16[128,128]{1,0:T(8,128)(2,1)} %bitcast.4, bf16[1024,128]{1,0:T(8,128)(2,1)} %bitcast.3, bf16[128,1024]{1,0:T(8,128)(2,1)} %ylm_hbm.1, f32[2]{0:T(128)} %weight_hbm.1, s32[8,128]{1,0:T(8,128)} %bitcast.5), custom_call_target="tpu_custom_call" | custom-call | tf_op jit(solution)/shard_map/dipole/pallas_call | solution.py:336
  30.8 1.3 %copy.7 = f32[8,16]{1,0:T(8,128)} copy(f32[8,16]{1,0:T(8,128)} %dipole.1) | data formatting | bytes 1024

commit v9 on v8

--- a/solution.py
+++ b/solution.py
@@ -23,7 +23,7 @@
     ((dx, dy, dc) for dx in range(NX) for dy in range(NY) for dc in range(NC) if (dx, dy, dc) != (0, 0, 0)),
     key=lambda o: -(ring(o[0], NX) + ring(o[1], NY)),
 )
-NEXT = 2
+NEXT = 3
 BY_ID = pl.DeviceIdType.LOGICAL
 
 
@@ -199,8 +199,8 @@
 
     far, step = jnp.where(zl < HALF // 2, HALF - 1, 0), jnp.where(zl < HALF // 2, -1, 1)
 
-    def give_pieces(own_k, both_from):
-        for k in range(HALF):
+    def give_pieces(own_k, steps, both_from):
+        for k in steps:
             for d in (2, 1, 3, 0):
                 if (k, d) == (own_k, 0):
                     continue
@@ -212,11 +212,11 @@
 
     @pl.when(edge)
     def _():
-        give_pieces(HALF - 1, NEXT)
+        give_pieces(HALF - 1, (1, 0, 2, 3), NEXT)
 
     @pl.when(jnp.logical_not(edge))
     def _():
-        give_pieces(HALF // 2, 0)
+        give_pieces(HALF // 2, range(HALF), 0)
 
     send(mine, m_full.at[block], out_sem.at[4], relay_recv, twin).start()
     m_full[block] = mine[...]
@@ -314,7 +314,11 @@
 
     @pl.when(edge)
     def _():
-        sent_pieces(6, 2 * NY)
+        sent_pieces(6, NY)
+
+    @pl.when(jnp.logical_not(edge))
+    def _():
+        sent_pieces(4, NY)
 
     pltpu.make_async_copy(recvbuf, recvbuf, end_recv).wait()
     row = jnp.sum(recvbuf[...], axis=0, keepdims=True)

time: 32.2 us -> 31.7 us (0.984)
  Pallas kernels: 30.8 us -> 30.3 us
    pallas_call x1, Pallas kernels: 30.8 us -> 30.3 us  [shards(): pl.pallas_call(kernel, out_shape=jax.ShapeDtypeStruct((nb // ANG, count /...]
where the time goes in v9:
time: 31.7 us; the launch traced here: 31.6 us
  Pallas kernels  30.3 us (96%)
  local copies, waits for them, and re-layouts  1.28 us (4%)
    pallas_call x1, Pallas kernels, shards(): pl.pallas_call(kernel, out_shape=jax.ShapeDtypeStruct((nb // ANG, count /...  30.3 us
    unnamed x1, local copies, waits for them, and re-layouts  1.28 us

profile of v9, /device:TPU:1, one launch (start us, length us, event | category | flops | bytes accessed | tf_op | source)
XLA Modules:
  0.0 31.6 jit_solution(9053129015592497460)
XLA Ops:
  0.0 30.3 %dipole.1 = f32[8,16]{1,0:T(8,128)} custom-call(bf16[128,128]{1,0:T(8,128)(2,1)} %bitcast.4, bf16[1024,128]{1,0:T(8,128)(2,1)} %bitcast.3, bf16[128,1024]{1,0:T(8,128)(2,1)} %ylm_hbm.1, f32[2]{0:T(128)} %weight_hbm.1, s32[8,128]{1,0:T(8,128)} %bitcast.5), custom_call_target="tpu_custom_call" | custom-call | tf_op jit(solution)/shard_map/dipole/pallas_call | solution.py:340
  30.3 1.3 %copy.7 = f32[8,16]{1,0:T(8,128)} copy(f32[8,16]{1,0:T(8,128)} %dipole.1) | data formatting | bytes 1024

commit v10 on v9

--- a/solution.py
+++ b/solution.py
@@ -75,7 +75,7 @@
 ):
     sendbufs, (recvbuf, *semaphores) = rest[:HALF], rest[HALF:]
     local_sem, out_sem, a_recv, f_recv, m_recv, relay_recv, end_send, end_recv, *signals = semaphores
-    here, both, all_here = signals
+    here, both, answer, all_here = signals
     ang, rad = lax.axis_index("ang"), lax.axis_index("rad")
     x, half, core, spot = lax.div(ang, 2), lax.rem(ang, 2), lax.rem(rad, NC), lax.div(rad, NC)
     zl, y = lax.div(spot, NY), lax.rem(spot, NY)
@@ -110,9 +110,15 @@
         )
 
     barrier = pltpu.get_barrier_semaphore()
-    lines = (rows_from, opposite, rows_to, *zl_peers, *x_peers, *y_peers, twin)
+    lines = (rows_from, rows_to, *zl_peers, *x_peers, *y_peers, twin)
+    late_edge, near_edge = edge & (half == 1), edge & (half == 0)
     for where in lines:
         signal(barrier, where)
+
+    @pl.when(jnp.logical_not(late_edge))
+    def _():
+        signal(barrier, opposite)
+
     loads = [
         pltpu.make_async_copy(ylm_hbm, ylm, local_sem.at[0]),
         pltpu.make_async_copy(order_hbm, order_ref, local_sem.at[3]),
@@ -123,7 +129,7 @@
     load_ylm, load_order, load_cont, load_bound, load_weight = loads
     for load in loads:
         load.start()
-    pl.semaphore_wait(barrier, len(lines))
+    pl.semaphore_wait(barrier, jnp.where(near_edge, len(lines), len(lines) + 1))
 
     quarter_to = piece_of(to_x, lax.div(z_other, HALF), lax.rem(z_other, HALF), y, 1 - core)[1]
     rows = send(
@@ -135,7 +141,11 @@
 
     across = send(bound_hbm, bound.at[ang], out_sem.at[1], a_recv.at[0], opposite)
 
-    @pl.when(half == 0)
+    @pl.when(late_edge)
+    def _():
+        signal(answer, opposite)
+
+    @pl.when((half == 0) & jnp.logical_not(edge))
     def _():
         across.start()
 
@@ -172,7 +182,11 @@
     for where in x_peers:
         send(bound_hbm, bound.at[ang], out_sem.at[2], a_recv.at[1], where).start()
 
-    @pl.when(half == 1)
+    @pl.when(near_edge)
+    def _():
+        pl.semaphore_wait(answer, 1)
+
+    @pl.when((half == 1) | edge)
     def _():
         across.start()
 
@@ -370,7 +384,7 @@
             dma,
             dma,
             dma,
-            *[pltpu.SemaphoreType.REGULAR] * 2,
+            *[pltpu.SemaphoreType.REGULAR] * 3,
             pltpu.SemaphoreType.REGULAR((3,)),
         ],
         compiler_params=pltpu.CompilerParams(collective_id=0, has_side_effects=True),

time: 31.7 us -> 32 us (level)
  no operation moved by 1% of the time
where the time goes in v10:
time: 32 us; the launch traced here: 31.9 us
  Pallas kernels  30.6 us (96%)
  local copies, waits for them, and re-layouts  1.28 us (4%)
    pallas_call x1, Pallas kernels, shards(): pl.pallas_call(kernel, out_shape=jax.ShapeDtypeStruct((nb // ANG, count /...  30.6 us
    unnamed x1, local copies, waits for them, and re-layouts  1.28 us

profile of v10, /device:TPU:1, one launch (start us, length us, event | category | flops | bytes accessed | tf_op | source)
XLA Modules:
  0.0 31.9 jit_solution(8618203666524796971)
XLA Ops:
  0.0 30.6 %dipole.1 = f32[8,16]{1,0:T(8,128)} custom-call(bf16[128,128]{1,0:T(8,128)(2,1)} %bitcast.4, bf16[1024,128]{1,0:T(8,128)(2,1)} %bitcast.3, bf16[128,1024]{1,0:T(8,128)(2,1)} %ylm_hbm.1, f32[2]{0:T(128)} %weight_hbm.1, s32[8,128]{1,0:T(8,128)} %bitcast.5), custom_call_target="tpu_custom_call" | custom-call | tf_op jit(solution)/shard_map/dipole/pallas_call | solution.py:354
  30.6 1.3 %copy.7 = f32[8,16]{1,0:T(8,128)} copy(f32[8,16]{1,0:T(8,128)} %dipole.1) | data formatting | bytes 1024

commit v11 on v9

--- a/solution.py
+++ b/solution.py
@@ -57,21 +57,23 @@
 
 def turned(block):
     rows, lanes = block.shape
-    row = lax.broadcasted_iota(jnp.int32, block.shape, 0)
-    group = lax.broadcasted_iota(jnp.int32, block.shape, 1) // 16
+    tiles = block.reshape(rows // 8, 8, lanes)
+    row = lax.broadcasted_iota(jnp.int32, (1, 8, lanes), 1)
+    group = lax.broadcasted_iota(jnp.int32, (1, 8, lanes), 2) // 16
     for s in (1, 2, 4):
-        below = pltpu.roll(pltpu.roll(block, rows - s, 0), 16 * s, 1)
-        above = pltpu.roll(pltpu.roll(block, s, 0), lanes - 16 * s, 1)
-        low_row, low_group = (row & s) == 0, (group & s) == 0
-        block = jnp.where(
-            low_row == low_group, block, jnp.where(low_row, below, above)
-        )
-    return block
+        low = jnp.broadcast_to((row & s) == 0, tiles.shape)
+        same = jnp.broadcast_to(((row ^ group) & s) == 0, tiles.shape)
+        below = pltpu.roll(pltpu.roll(tiles, 8 - s, 1), 16 * s, 2)
+        if 2 * s < 8:
+            above = pltpu.roll(pltpu.roll(tiles, s, 1), lanes - 16 * s, 2)
+            below = jnp.where(low, below, above)
+        tiles = jnp.where(same, tiles, below)
+    return tiles.reshape(rows, lanes)
 
 
 def kernel(
     bound_hbm, cont_hbm, ylm_hbm, weight_hbm, order_hbm, out_ref,
-    bound, cont, ylm, order_ref, weight_ref, ys, ncol, z_ref, mine, m_full, cont_t, *rest
+    bound, cont, ylm, order_ref, weight_ref, ys, ncol, z_ref, mine, m_full, early_d, cont_t, *rest
 ):
     sendbufs, (recvbuf, *semaphores) = rest[:HALF], rest[HALF:]
     local_sem, out_sem, a_recv, f_recv, m_recv, relay_recv, end_send, end_recv, *signals = semaphores
@@ -208,7 +210,7 @@
                 send(mine, m_full.at[block], out_sem.at[3], m_recv.at[spot], where).start()
                 if both_from and own_k - k >= both_from:
                     where = where + 1 - 2 * core
-                    send(mine, m_full.at[block], out_sem.at[6], relay_recv, where).start()
+                    send(mine, m_full.at[block], out_sem.at[6], relay_recv.at[1], where).start()
 
     @pl.when(edge)
     def _():
@@ -218,7 +220,8 @@
     def _():
         give_pieces(HALF // 2, range(HALF), 0)
 
-    send(mine, m_full.at[block], out_sem.at[4], relay_recv, twin).start()
+    when = jnp.where(edge, 1, 0)
+    send(mine, m_full.at[block], out_sem.at[4], relay_recv.at[when], twin).start()
     m_full[block] = mine[...]
 
     signal(all_here.at[0], opposite)
@@ -230,7 +233,7 @@
     for where in x_peers:
         signal(all_here.at[1], where)
 
-    def pass_on(start, end, limit):
+    def pass_on(start, end, limit, when):
         def act(i):
             @pl.when(i != spot)
             def _():
@@ -239,27 +242,39 @@
 
                 @pl.when(jnp.abs(lax.div(i, NY) - zl) < limit)
                 def _():
-                    send(there, there, out_sem.at[4], relay_recv, twin).start()
+                    send(there, there, out_sem.at[4], relay_recv.at[when], twin).start()
 
         each(start, end, act)
 
-    pass_on(NY, spots - NY, spots)
-    pass_on(0, NY, NEXT)
-    pass_on(spots - NY, spots, NEXT)
+    def passed(when):
+        part = m_full.at[pl.ds(0, spots // 2)]
+        send(part, part, out_sem.at[4], relay_recv.at[when], twin).wait_recv()
+
+    def product(side):
+        left = jnp.concatenate([bound[2 * i + side] for i in range(NX)], axis=1)
+        right = [
+            m_full[pl.ds((2 * i + side) * (RAD // ANG), RAD // ANG)].reshape(PTS, PTS)
+            for i in range(NX)
+        ]
+        right = jnp.concatenate(right, axis=0)
+        return jnp.dot(left, right, preferred_element_type=F32)
+
+    pass_on(NY, spots - NY, spots, 0)
     load_bound.wait()
     load_weight.wait()
     three = bound.at[pl.ds(0, NX - 1)]
-    for i in (1, 2):
-        send(three, three, out_sem.at[2], a_recv.at[i], twin).wait_recv()
+    send(three, three, out_sem.at[2], a_recv.at[1], twin).wait_recv()
+    passed(0)
+    early_d[...] = product(half)
+    pass_on(0, NY, NEXT, 1)
+    pass_on(spots - NY, spots, NEXT, 1)
+    send(three, three, out_sem.at[2], a_recv.at[2], twin).wait_recv()
     pl.semaphore_wait(all_here.at[1], NX - 1)
     signal(all_here.at[2], twin)
-    bound_all = jnp.concatenate([bound[i] for i in range(ANG)], axis=1)
-    half_m = m_full.at[pl.ds(0, spots)]
-    send(half_m, half_m, out_sem.at[4], relay_recv, twin).wait_recv()
+    passed(1)
     pl.semaphore_wait(all_here.at[2], 1)
 
-    operator = m_full[...].reshape(PTS * ANG, PTS)
-    d = jnp.dot(bound_all, operator, preferred_element_type=F32)
+    d = early_d[...] + product(1 - half)
     nb = d.shape[0] // shells
     weighted = [d[r * nb : (r + 1) * nb] * weight_ref[r] for r in range(shells)]
     wide = jnp.concatenate(weighted, axis=1).astype(BF16)
@@ -304,11 +319,11 @@
     for i in (2, 5):
         send(three, three, out_sem.at[i], a_recv.at[1], twin).wait_send()
     own_m = m_full.at[pl.ds(0, spots - 1)]
-    send(own_m, own_m, out_sem.at[3], relay_recv, twin).wait_send()
+    send(own_m, own_m, out_sem.at[3], relay_recv.at[0], twin).wait_send()
 
     def sent_pieces(i, n):
         part = m_full.at[pl.ds(0, n)]
-        send(part, part, out_sem.at[i], relay_recv, twin).wait_send()
+        send(part, part, out_sem.at[i], relay_recv.at[0], twin).wait_send()
 
     sent_pieces(4, spots - NY)
 
@@ -359,6 +374,7 @@
             pltpu.VMEM((TOTAL, points), BF16),
             pltpu.VMEM((PIECE, points), BF16),
             pltpu.VMEM((RAD, PIECE, points), BF16),
+            pltpu.VMEM((shells * nb, points), F32),
             pltpu.VMEM((shells * points, count), BF16),
             *[pltpu.VMEM((64, 128), F32)] * HALF,
             pltpu.VMEM((ANG * RAD, 128), F32),
@@ -367,7 +383,7 @@
             dma((3,)),
             dma,
             dma((RAD // NC,)),
-            dma,
+            dma((2,)),
             dma,
             dma,
             *[pltpu.SemaphoreType.REGULAR] * 2,

time: 31.7 us -> 31.6 us (level)
  no operation moved by 1% of the time
where the time goes in v11:
time: 31.6 us; the launch traced here: 31.5 us
  Pallas kernels  30.2 us (96%)
  local copies, waits for them, and re-layouts  1.28 us (4%)
    pallas_call x1, Pallas kernels, shards(): pl.pallas_call(kernel, out_shape=jax.ShapeDtypeStruct((nb // ANG, count /...  30.2 us
    unnamed x1, local copies, waits for them, and re-layouts  1.28 us

profile of v11, /device:TPU:1, one launch (start us, length us, event | category | flops | bytes accessed | tf_op | source)
XLA Modules:
  0.0 31.5 jit_solution(17465892936503078476)
XLA Ops:
  0.0 30.2 %dipole.1 = f32[8,16]{1,0:T(8,128)} custom-call(bf16[128,128]{1,0:T(8,128)(2,1)} %bitcast.4, bf16[1024,128]{1,0:T(8,128)(2,1)} %bitcast.3, bf16[128,1024]{1,0:T(8,128)(2,1)} %ylm_hbm.1, f32[2]{0:T(128)} %weight_hbm.1, s32[8,128]{1,0:T(8,128)} %bitcast.5), custom_call_target="tpu_custom_call" | custom-call | tf_op jit(solution)/shard_map/dipole/pallas_call | solution.py:355
  30.2 1.3 %copy.7 = f32[8,16]{1,0:T(8,128)} copy(f32[8,16]{1,0:T(8,128)} %dipole.1) | data formatting | bytes 1024

commit v12 on v11

--- a/solution.py
+++ b/solution.py
@@ -266,8 +266,9 @@
     send(three, three, out_sem.at[2], a_recv.at[1], twin).wait_recv()
     passed(0)
     early_d[...] = product(half)
-    pass_on(0, NY, NEXT, 1)
-    pass_on(spots - NY, spots, NEXT, 1)
+    near = jnp.where(zl < HALF // 2, 0, spots - NY)
+    for start in (near, spots - NY - near):
+        pass_on(start, start + NY, NEXT, 1)
     send(three, three, out_sem.at[2], a_recv.at[2], twin).wait_recv()
     pl.semaphore_wait(all_here.at[1], NX - 1)
     signal(all_here.at[2], twin)

time: 31.6 us -> 31.6 us (level)
  no operation moved by 1% of the time
where the time goes in v12:
time: 31.6 us; the launch traced here: 31.5 us
  Pallas kernels  30.3 us (96%)
  local copies, waits for them, and re-layouts  1.28 us (4%)
    pallas_call x1, Pallas kernels, shards(): pl.pallas_call(kernel, out_shape=jax.ShapeDtypeStruct((nb // ANG, count /...  30.3 us
    unnamed x1, local copies, waits for them, and re-layouts  1.28 us

profile of v12, /device:TPU:1, one launch (start us, length us, event | category | flops | bytes accessed | tf_op | source)
XLA Modules:
  0.0 31.5 jit_solution(5030284867093552294)
XLA Ops:
  0.0 30.3 %dipole.1 = f32[8,16]{1,0:T(8,128)} custom-call(bf16[128,128]{1,0:T(8,128)(2,1)} %bitcast.4, bf16[1024,128]{1,0:T(8,128)(2,1)} %bitcast.3, bf16[128,1024]{1,0:T(8,128)(2,1)} %ylm_hbm.1, f32[2]{0:T(128)} %weight_hbm.1, s32[8,128]{1,0:T(8,128)} %bitcast.5), custom_call_target="tpu_custom_call" | custom-call | tf_op jit(solution)/shard_map/dipole/pallas_call | solution.py:356
  30.3 1.3 %copy.7 = f32[8,16]{1,0:T(8,128)} copy(f32[8,16]{1,0:T(8,128)} %dipole.1) | data formatting | bytes 1024

commit v13 on v12

--- a/solution.py
+++ b/solution.py
@@ -23,7 +23,7 @@
     ((dx, dy, dc) for dx in range(NX) for dy in range(NY) for dc in range(NC) if (dx, dy, dc) != (0, 0, 0)),
     key=lambda o: -(ring(o[0], NX) + ring(o[1], NY)),
 )
-NEXT = 3
+NEXT = 2
 BY_ID = pl.DeviceIdType.LOGICAL
 
 
@@ -208,7 +208,7 @@
                     continue
                 where = ang * RAD + (far + step * k) * NY * NC + lax.rem(y + d, NY) * NC + core
                 send(mine, m_full.at[block], out_sem.at[3], m_recv.at[spot], where).start()
-                if both_from and own_k - k >= both_from:
+                if both_from and own_k - k == both_from:
                     where = where + 1 - 2 * core
                     send(mine, m_full.at[block], out_sem.at[6], relay_recv.at[1], where).start()
 
@@ -233,14 +233,14 @@
     for where in x_peers:
         signal(all_here.at[1], where)
 
-    def pass_on(start, end, limit, when):
+    def pass_on(start, end, not_at, when):
         def act(i):
             @pl.when(i != spot)
             def _():
                 there = m_full.at[block_of(i)]
                 send(there, there, out_sem.at[4], m_recv.at[i], twin).wait_recv()
 
-                @pl.when(jnp.abs(lax.div(i, NY) - zl) < limit)
+                @pl.when(jnp.abs(lax.div(i, NY) - zl) != not_at)
                 def _():
                     send(there, there, out_sem.at[4], relay_recv.at[when], twin).start()
 
@@ -330,11 +330,8 @@
 
     @pl.when(edge)
     def _():
+        sent_pieces(4, NY)
         sent_pieces(6, NY)
-
-    @pl.when(jnp.logical_not(edge))
-    def _():
-        sent_pieces(4, NY)
 
     pltpu.make_async_copy(recvbuf, recvbuf, end_recv).wait()
     row = jnp.sum(recvbuf[...], axis=0, keepdims=True)

time: 31.6 us -> 32.5 us (1.028)
  Pallas kernels: 30.3 us -> 31.1 us
    pallas_call x1, Pallas kernels: 30.3 us -> 31.1 us  [shards(): pl.pallas_call(kernel, out_shape=jax.ShapeDtypeStruct((nb // ANG, count /...]
where the time goes in v13:
time: 32.5 us; the launch traced here: 32.4 us
  Pallas kernels  31.1 us (96%)
  local copies, waits for them, and re-layouts  1.28 us (4%)
    pallas_call x1, Pallas kernels, shards(): pl.pallas_call(kernel, out_shape=jax.ShapeDtypeStruct((nb // ANG, count /...  31.1 us
    unnamed x1, local copies, waits for them, and re-layouts  1.28 us

profile of v13, /device:TPU:1, one launch (start us, length us, event | category | flops | bytes accessed | tf_op | source)
XLA Modules:
  0.0 32.4 jit_solution(8752277599318097378)
XLA Ops:
  0.0 31.1 %dipole.1 = f32[8,16]{1,0:T(8,128)} custom-call(bf16[128,128]{1,0:T(8,128)(2,1)} %bitcast.4, bf16[1024,128]{1,0:T(8,128)(2,1)} %bitcast.3, bf16[128,1024]{1,0:T(8,128)(2,1)} %ylm_hbm.1, f32[2]{0:T(128)} %weight_hbm.1, s32[8,128]{1,0:T(8,128)} %bitcast.5), custom_call_target="tpu_custom_call" | custom-call | tf_op jit(solution)/shard_map/dipole/pallas_call | solution.py:353
  31.1 1.3 %copy.7 = f32[8,16]{1,0:T(8,128)} copy(f32[8,16]{1,0:T(8,128)} %dipole.1) | data formatting | bytes 1024

commit v14 on v13

--- a/solution.py
+++ b/solution.py
@@ -23,7 +23,6 @@
     ((dx, dy, dc) for dx in range(NX) for dy in range(NY) for dc in range(NC) if (dx, dy, dc) != (0, 0, 0)),
     key=lambda o: -(ring(o[0], NX) + ring(o[1], NY)),
 )
-NEXT = 2
 BY_ID = pl.DeviceIdType.LOGICAL
 
 
@@ -201,24 +200,20 @@
 
     far, step = jnp.where(zl < HALF // 2, HALF - 1, 0), jnp.where(zl < HALF // 2, -1, 1)
 
-    def give_pieces(own_k, steps, both_from):
+    def give_pieces(own_k, steps):
         for k in steps:
             for d in (2, 1, 3, 0):
-                if (k, d) == (own_k, 0):
-                    continue
-                where = ang * RAD + (far + step * k) * NY * NC + lax.rem(y + d, NY) * NC + core
-                send(mine, m_full.at[block], out_sem.at[3], m_recv.at[spot], where).start()
-                if both_from and own_k - k == both_from:
-                    where = where + 1 - 2 * core
-                    send(mine, m_full.at[block], out_sem.at[6], relay_recv.at[1], where).start()
+                if (k, d) != (own_k, 0):
+                    where = ang * RAD + (far + step * k) * NY * NC + lax.rem(y + d, NY) * NC + core
+                    send(mine, m_full.at[block], out_sem.at[3], m_recv.at[spot], where).start()
 
     @pl.when(edge)
     def _():
-        give_pieces(HALF - 1, (1, 0, 2, 3), NEXT)
+        give_pieces(HALF - 1, (1, 0, 2, 3))
 
     @pl.when(jnp.logical_not(edge))
     def _():
-        give_pieces(HALF // 2, range(HALF), 0)
+        give_pieces(HALF // 2, range(HALF))
 
     when = jnp.where(edge, 1, 0)
     send(mine, m_full.at[block], out_sem.at[4], relay_recv.at[when], twin).start()
@@ -233,16 +228,13 @@
     for where in x_peers:
         signal(all_here.at[1], where)
 
-    def pass_on(start, end, not_at, when):
+    def pass_on(start, end, when):
         def act(i):
             @pl.when(i != spot)
             def _():
                 there = m_full.at[block_of(i)]
                 send(there, there, out_sem.at[4], m_recv.at[i], twin).wait_recv()
-
-                @pl.when(jnp.abs(lax.div(i, NY) - zl) != not_at)
-                def _():
-                    send(there, there, out_sem.at[4], relay_recv.at[when], twin).start()
+                send(there, there, out_sem.at[4], relay_recv.at[when], twin).start()
 
         each(start, end, act)
 
@@ -259,7 +251,7 @@
         right = jnp.concatenate(right, axis=0)
         return jnp.dot(left, right, preferred_element_type=F32)
 
-    pass_on(NY, spots - NY, spots, 0)
+    pass_on(NY, spots - NY, 0)
     load_bound.wait()
     load_weight.wait()
     three = bound.at[pl.ds(0, NX - 1)]
@@ -268,7 +260,7 @@
     early_d[...] = product(half)
     near = jnp.where(zl < HALF // 2, 0, spots - NY)
     for start in (near, spots - NY - near):
-        pass_on(start, start + NY, NEXT, 1)
+        pass_on(start, start + NY, 1)
     send(three, three, out_sem.at[2], a_recv.at[2], twin).wait_recv()
     pl.semaphore_wait(all_here.at[1], NX - 1)
     signal(all_here.at[2], twin)
@@ -326,13 +318,7 @@
         part = m_full.at[pl.ds(0, n)]
         send(part, part, out_sem.at[i], relay_recv.at[0], twin).wait_send()
 
-    sent_pieces(4, spots - NY)
-
-    @pl.when(edge)
-    def _():
-        sent_pieces(4, NY)
-        sent_pieces(6, NY)
-
+    sent_pieces(4, spots)
     pltpu.make_async_copy(recvbuf, recvbuf, end_recv).wait()
     row = jnp.sum(recvbuf[...], axis=0, keepdims=True)
     wide_row = jnp.broadcast_to(row, (8, 128))
@@ -377,7 +363,7 @@
             *[pltpu.VMEM((64, 128), F32)] * HALF,
             pltpu.VMEM((ANG * RAD, 128), F32),
             dma((5,)),
-            dma((7,)),
+            dma((6,)),
             dma((3,)),
             dma,
             dma((RAD // NC,)),

time: 32.5 us -> 31.8 us (0.978)
  Pallas kernels: 31.1 us -> 30.4 us
    pallas_call x1, Pallas kernels: 31.1 us -> 30.4 us  [shards(): pl.pallas_call(kernel, out_shape=jax.ShapeDtypeStruct((nb // ANG, count /...]
where the time goes in v14:
time: 31.8 us; the launch traced here: 31.7 us
  Pallas kernels  30.4 us (96%)
  local copies, waits for them, and re-layouts  1.28 us (4%)
    pallas_call x1, Pallas kernels, shards(): pl.pallas_call(kernel, out_shape=jax.ShapeDtypeStruct((nb // ANG, count /...  30.4 us
    unnamed x1, local copies, waits for them, and re-layouts  1.28 us

profile of v14, /device:TPU:1, one launch (start us, length us, event | category | flops | bytes accessed | tf_op | source)
XLA Modules:
  0.0 31.7 jit_solution(8719926775780795979)
XLA Ops:
  0.0 30.4 %dipole.1 = f32[8,16]{1,0:T(8,128)} custom-call(bf16[128,128]{1,0:T(8,128)(2,1)} %bitcast.4, bf16[1024,128]{1,0:T(8,128)(2,1)} %bitcast.3, bf16[128,1024]{1,0:T(8,128)(2,1)} %ylm_hbm.1, f32[2]{0:T(128)} %weight_hbm.1, s32[8,128]{1,0:T(8,128)} %bitcast.5), custom_call_target="tpu_custom_call" | custom-call | tf_op jit(solution)/shard_map/dipole/pallas_call | solution.py:339
  30.4 1.3 %copy.7 = f32[8,16]{1,0:T(8,128)} copy(f32[8,16]{1,0:T(8,128)} %dipole.1) | data formatting | bytes 1024

commit v15 on v11

--- a/solution.py
+++ b/solution.py
@@ -137,10 +137,6 @@
 
     across = send(bound_hbm, bound.at[ang], out_sem.at[1], a_recv.at[0], opposite)
 
-    @pl.when(half == 0)
-    def _():
-        across.start()
-
     for where in y_peers:
         signal(here, where)
 
@@ -170,7 +166,14 @@
         ).astype(BF16)
         return carry
 
-    lax.fori_loop(0, TOTAL // 128, couple, 0)
+    middle = TOTAL // 256
+    lax.fori_loop(0, middle, couple, 0)
+
+    @pl.when(half == 0)
+    def _():
+        across.start()
+
+    lax.fori_loop(middle, TOTAL // 128, couple, 0)
     for where in x_peers:
         send(bound_hbm, bound.at[ang], out_sem.at[2], a_recv.at[1], where).start()
 

time: 31.6 us -> 31.3 us (level)
  no operation moved by 1% of the time
where the time goes in v15:
time: 31.3 us; the launch traced here: 31.2 us
  Pallas kernels  29.9 us (96%)
  local copies, waits for them, and re-layouts  1.28 us (4%)
    pallas_call x1, Pallas kernels, shards(): pl.pallas_call(kernel, out_shape=jax.ShapeDtypeStruct((nb // ANG, count /...  29.9 us
    unnamed x1, local copies, waits for them, and re-layouts  1.28 us

profile of v15, /device:TPU:1, one launch (start us, length us, event | category | flops | bytes accessed | tf_op | source)
XLA Modules:
  0.0 31.2 jit_solution(17749996744285084076)
XLA Ops:
  0.0 29.9 %dipole.1 = f32[8,16]{1,0:T(8,128)} custom-call(bf16[128,128]{1,0:T(8,128)(2,1)} %bitcast.4, bf16[1024,128]{1,0:T(8,128)(2,1)} %bitcast.3, bf16[128,1024]{1,0:T(8,128)(2,1)} %ylm_hbm.1, f32[2]{0:T(128)} %weight_hbm.1, s32[8,128]{1,0:T(8,128)} %bitcast.5), custom_call_target="tpu_custom_call" | custom-call | tf_op jit(solution)/shard_map/dipole/pallas_call | solution.py:358
  29.9 1.3 %copy.7 = f32[8,16]{1,0:T(8,128)} copy(f32[8,16]{1,0:T(8,128)} %dipole.1) | data formatting | bytes 1024

commit v16 on v15

--- a/solution.py
+++ b/solution.py
@@ -269,8 +269,9 @@
     send(three, three, out_sem.at[2], a_recv.at[1], twin).wait_recv()
     passed(0)
     early_d[...] = product(half)
-    pass_on(0, NY, NEXT, 1)
-    pass_on(spots - NY, spots, NEXT, 1)
+    near = jnp.where(zl < HALF // 2, 0, spots - NY)
+    for start in (near, spots - NY - near):
+        pass_on(start, start + NY, NEXT, 1)
     send(three, three, out_sem.at[2], a_recv.at[2], twin).wait_recv()
     pl.semaphore_wait(all_here.at[1], NX - 1)
     signal(all_here.at[2], twin)

time: 31.3 us -> 31.3 us (level)
  no operation moved by 1% of the time
where the time goes in v16:
time: 31.3 us; the launch traced here: 31.2 us
  Pallas kernels  29.9 us (96%)
  local copies, waits for them, and re-layouts  1.28 us (4%)
    pallas_call x1, Pallas kernels, shards(): pl.pallas_call(kernel, out_shape=jax.ShapeDtypeStruct((nb // ANG, count /...  29.9 us
    unnamed x1, local copies, waits for them, and re-layouts  1.28 us

profile of v16, /device:TPU:1, one launch (start us, length us, event | category | flops | bytes accessed | tf_op | source)
XLA Modules:
  0.0 31.2 jit_solution(5915911827901287016)
XLA Ops:
  0.0 29.9 %dipole.1 = f32[8,16]{1,0:T(8,128)} custom-call(bf16[128,128]{1,0:T(8,128)(2,1)} %bitcast.4, bf16[1024,128]{1,0:T(8,128)(2,1)} %bitcast.3, bf16[128,1024]{1,0:T(8,128)(2,1)} %ylm_hbm.1, f32[2]{0:T(128)} %weight_hbm.1, s32[8,128]{1,0:T(8,128)} %bitcast.5), custom_call_target="tpu_custom_call" | custom-call | tf_op jit(solution)/shard_map/dipole/pallas_call | solution.py:359
  29.9 1.3 %copy.7 = f32[8,16]{1,0:T(8,128)} copy(f32[8,16]{1,0:T(8,128)} %dipole.1) | data formatting | bytes 1024
